TPU v7x, 32 devices: a whole 2x2x4 slice. The times are simulated.
32 devices in a mesh: ctx: 8 (over y, x, core), head: 4 (over z).
Axes of the slice: x: 2, y: 2, z: 4, core: 2. Of those that a mesh axis runs over, the one named last changes fastest.
Arguments:
- query_key: bfloat16 [4096, 1024], P('ctx', 'head'), may hold values from -6 to 6
- values: bfloat16 [4096, 4096], P('ctx', 'head'), may hold values from -6 to 6
- out_grad: bfloat16 [4096, 4096], P('ctx', 'head'), may hold values from -6 to 6
- out_weight: bfloat16 [4096, 4096], P('head'), may hold values from -0.09375 to 0.09375
- doc_lengths: int32 [32], replicated, may hold values from 1 to 2048, 4096 in all
Outputs:
- qk_grad: bfloat16 [4096, 1024], P('ctx', 'head')
- value_grad: bfloat16 [4096, 4096], P('ctx', 'head')
- proj_grad: float32 [4096, 4096], P('head', 'ctx')
Inputs may be any that keep to these rules, and one draw needn't show every extreme that they name: `doc_lengths`: the documents fill all 4096 positions in order; the longest has exactly 2048 tokens.
All inputs are finite; a program needn't handle non-finite values.
Results may differ from a plain program's by a relative error of at most 0.0068.
Values may be sent and summed in bfloat16 or wider, within the bound.
A program may use at most 128 MiB of HBM per device.

v0:
```python
import math

import jax
import jax.numpy as jnp
from jax import lax
from jax.sharding import PartitionSpec as P

HEAD = 128
QK = 16
SPAN = 4


quad_scale = 0.25 / math.sqrt(2.0)
highest = lax.Precision.HIGHEST


def shifted(value, axis, steps):
    count = lax.axis_size(axis)
    leading, last = (max(0, -steps), min(count, count - steps))
    return lax.ppermute(value, axis, [(source, source + steps) for source in range(leading, last)])


def shortened(x):

    def short(part):
        return part.astype(jnp.bfloat16) if part.dtype == jnp.float32 else part

    return jax.tree.map(short, x)


def features(points):
    feat_width = points.shape[-1]
    constant = jnp.ones(points.shape[:-1] + (1,), jnp.float32)
    products = (points[..., :, None] * points[..., None, :]).reshape(
        points.shape[:-1] + (feat_width * feat_width,)
    )
    return jnp.concatenate([constant, points * 0.5, products * quad_scale], axis=-1)


def feature_grad(grad_feat, points):
    feat_width = points.shape[-1]
    linear = grad_feat[..., 1 : 1 + feat_width] * 0.5
    square = grad_feat[..., 1 + feat_width :].reshape(points.shape[:-1] + (feat_width, feat_width))
    paired = square + jnp.swapaxes(square, -1, -2)
    return linear + quad_scale * jnp.sum(paired * points[..., None, :], axis=-1)


def segment_ids(doc_lengths, positions):
    starts = jnp.cumsum(doc_lengths, dtype=jnp.int32) - doc_lengths
    return jnp.sum((starts[None, :] <= positions[:, None]).astype(jnp.int32), axis=1) - 1


def carry_doc(earlier, latter):
    retained = 1.0 - latter[2]
    return (
        latter[0] + retained * earlier[0],
        latter[1] + retained * earlier[1],
        jnp.maximum(earlier[2], latter[2]),
    )


def on_device(query_key, values, out_grad, out_weight, doc_lengths):
    tokens = query_key.shape[0]
    head_count = out_weight.shape[0] // HEAD
    row_block = min(tokens, 512)
    offset = lax.axis_index("ctx") * tokens
    positions = offset + jnp.arange(tokens, dtype=jnp.int32)
    segment = segment_ids(doc_lengths, positions)
    open_before = segment_ids(doc_lengths, jnp.reshape(offset - 1, (1,)))[0]
    open_after = segment[tokens - 1]
    restart = (open_after != open_before).astype(jnp.float32)
    carried = (segment == open_before).astype(jnp.float32)
    ending = (segment == open_after).astype(jnp.float32)
    paired = query_key.reshape(tokens, head_count, 2, QK).transpose(1, 2, 0, 3)
    queries = paired[:, 0]
    keys_all = paired[:, 1]
    value_rows = values.reshape(tokens, head_count, HEAD).transpose(1, 0, 2)
    query_feat = features(queries.astype(jnp.float32)).astype(jnp.bfloat16)
    key_feat = features(keys_all.astype(jnp.float32)).astype(jnp.bfloat16)
    ending_feat = jnp.where(ending[None, :, None] > 0.5, key_feat, jnp.zeros_like(key_feat))
    state_local = jnp.einsum(
        "htf,htd->hfd", ending_feat, value_rows, preferred_element_type=jnp.float32
    )
    norm_local = jnp.sum(ending_feat.astype(jnp.float32), axis=1)
    identity = (jnp.zeros_like(state_local), jnp.zeros_like(norm_local), jnp.zeros((), jnp.float32))
    local_fwd = (state_local, norm_local, restart)
    incoming = identity
    for repeat_idx in range(SPAN):
        incoming = shifted(carry_doc(incoming, local_fwd), "ctx", 1)
    state_b = incoming[0].astype(jnp.bfloat16)
    norm_in = incoming[1]
    full_out = lax.all_gather(out_grad, "head", axis=1, tiled=True)
    out_rows = lax.dot_general(
        full_out, out_weight, (((1,), (1,)), ((), ())), preferred_element_type=jnp.float32
    )
    grads_out = out_rows.reshape(tokens, head_count, HEAD).transpose(1, 0, 2)
    places = jnp.arange(tokens, dtype=jnp.int32)
    row_span = slice(0, row_block)
    scores = (
        jnp.einsum("hid,hjd->hij", queries, keys_all, preferred_element_type=jnp.float32) * 0.25
    )
    visible = (places[None, :] <= places[row_span, None]) & (
        segment[row_span, None] == segment[None, :]
    )
    weight = jnp.where(visible[None], 1.0 + scores + 0.5 * scores * scores, 0.0)
    weight_b = weight.astype(jnp.bfloat16)
    from_state = jnp.einsum("hif,hfd->hid", query_feat, state_b, preferred_element_type=jnp.float32)
    numerator = (
        jnp.einsum("hij,hjd->hid", weight_b, value_rows, preferred_element_type=jnp.float32)
        + carried[None, :, None] * from_state
    )
    denominator = jnp.sum(weight, axis=2) + carried[None, :] * jnp.einsum(
        "hif,hf->hi", query_feat.astype(jnp.float32), norm_in, precision=highest
    )
    attended = numerator / denominator[:, :, None]
    attended_list = attended.astype(jnp.bfloat16)
    den_grad = -jnp.sum(grads_out * attended, axis=2) / denominator
    num_grad = (grads_out / denominator[:, :, None]).astype(jnp.bfloat16)
    mix_grad = (
        jnp.einsum("hid,hjd->hij", num_grad, value_rows, preferred_element_type=jnp.float32)
        + den_grad[:, :, None]
    )
    score_grad = jnp.where(visible[None], mix_grad * (1.0 + scores), 0.0).astype(jnp.bfloat16)
    value_grad = jnp.einsum("hij,hid->hjd", weight_b, num_grad, preferred_element_type=jnp.float32)
    key_grad = 0.25 * jnp.einsum(
        "hij,hid->hjd", score_grad, queries, preferred_element_type=jnp.float32
    )
    feat_grad = carried[None, :, None] * (
        jnp.einsum("hid,hfd->hif", num_grad, state_b, preferred_element_type=jnp.float32)
        + den_grad[:, :, None] * norm_in[:, None, :]
    )
    query_list = 0.25 * jnp.einsum(
        "hij,hjd->hid", score_grad, keys_all, preferred_element_type=jnp.float32
    ) + feature_grad(feat_grad, queries.astype(jnp.float32))
    near_feat = jnp.where(carried[None, :, None] > 0.5, query_feat, jnp.zeros_like(query_feat))
    adj_local = jnp.einsum("hif,hid->hfd", near_feat, num_grad, preferred_element_type=jnp.float32)
    nadj_local = jnp.einsum(
        "hif,hi->hf", near_feat.astype(jnp.float32), den_grad, precision=highest
    )
    attended_all = attended_list.transpose(1, 0, 2).reshape(tokens, head_count * HEAD)
    term = lax.dot_general(
        attended_all, full_out, (((0,), (0,)), ((), ())), preferred_element_type=jnp.float32
    )
    proj_grad = lax.psum_scatter(term, "ctx", scatter_dimension=1, tiled=True)
    local_back = (adj_local, nadj_local, restart)
    outgoing = identity
    for repeat_idx in range(SPAN):
        outgoing = shifted(shortened(carry_doc(outgoing, local_back)), "ctx", -1)
    adjoint_b = outgoing[0].astype(jnp.bfloat16)
    ending_col = ending[None, :, None]
    value_grad = value_grad + ending_col * jnp.einsum(
        "htf,hfd->htd", key_feat, adjoint_b, preferred_element_type=jnp.float32
    )
    key_feat_grad = ending_col * (
        jnp.einsum("htd,hfd->htf", value_rows, adjoint_b, preferred_element_type=jnp.float32)
        + outgoing[1][:, None, :]
    )
    key_grad = key_grad + feature_grad(key_feat_grad, keys_all.astype(jnp.float32))
    qk_grad = (
        jnp.stack([query_list, key_grad], axis=2)
        .transpose(1, 0, 2, 3)
        .reshape(tokens, head_count * 2 * QK)
        .astype(jnp.bfloat16)
    )
    value_out = (
        value_grad.transpose(1, 0, 2).reshape(tokens, head_count * HEAD).astype(jnp.bfloat16)
    )
    return (qk_grad, value_out, proj_grad)


def solution(mesh):
    placed = (P("ctx", "head"), P("ctx", "head"), P("ctx", "head"), P("head", None), P())
    return jax.shard_map(
        on_device,
        mesh=mesh,
        in_specs=placed,
        out_specs=(P("ctx", "head"), P("ctx", "head"), P("head", "ctx")),
        check_vma=False,
    )
```

profile of v0, /device:TPU:0, one launch (start us, length us, event | category | flops | bytes accessed | tf_op | source)
XLA Modules:
  0.0 244.7 jit_solution(4996594267728297888)
XLA Ops:
  14.8 2.3 broadcast_add_fusion
  17.3 2.5 %collective-permute-start.4 = (f32[8,273,128]{2,0,1:T(8,128)S(1)}, f32[8,273,128]{2,0,1:T(8,128)S(1)}, u32[]{:S(2)}, u32[]{:S(2)}) collective-permute-start(f32[8,273,128]{2,0,1:T(8,128)S(1)} %copy.122), channel_id=1, source_target_pairs={{0,4},{4,8},{8,12},{12,16},{16,20},{20,24},{24,28},{1,5},{5,9},{9,... | collective-permute-start | bytes 3354632 | tf_op jit(solution)/shard_map/ppermute | solution.py:20
  20.9 4.4 %collective-permute-start = (f32[8,273]{1,0:T(8,128)S(1)}, f32[8,273]{1,0:T(8,128)S(1)}, u32[]{:S(2)}, u32[]{:S(2)}) collective-permute-start(f32[8,273]{1,0:T(8,128)S(1)} %broadcast_add_fusion.1), channel_id=1, source_target_pairs={{0,4},{4,8},{8,12},{12,16},{16,20},{20,24},{24,28},{1,5},{5,9},{9,... | collective-permute-start | bytes 26216 | tf_op jit(solution)/shard_map/ppermute | solution.py:20
  25.6 11.3 %collective-permute-start.5 = (f32[8,273,128]{2,0,1:T(8,128)S(1)}, f32[8,273,128]{2,0,1:T(8,128)S(1)}, u32[]{:S(2)}, u32[]{:S(2)}) collective-permute-start(f32[8,273,128]{2,0,1:T(8,128)S(1)} %multiply_add_fusion.3), channel_id=1, source_target_pairs={{0,4},{4,8},{8,12},{12,16},{16,20},{20,24},{24,28},{1,5},{5,9},{9,... | collective-permute-start | bytes 3354632 | tf_op jit(solution)/shard_map/ppermute | solution.py:20
  37.2 4.5 %collective-permute-start.1 = (f32[8,273]{1,0:T(8,128)S(1)}, f32[8,273]{1,0:T(8,128)S(1)}, u32[]{:S(2)}, u32[]{:S(2)}) collective-permute-start(f32[8,273]{1,0:T(8,128)S(1)} %multiply_add_fusion.6), channel_id=1, source_target_pairs={{0,4},{4,8},{8,12},{12,16},{16,20},{20,24},{24,28},{1,5},{5,9},{9,... | collective-permute-start | bytes 26216 | tf_op jit(solution)/shard_map/ppermute | solution.py:20
  41.7 2.8 %fusion.1 = (f32[8,512]{1,0:T(8,128)S(1)}, f32[8,512,512]{1,2,0:T(8,128)S(1)}) fusion(pred[512,512]{0,1:T(8,128)(4,1)S(1)} %fusion.15, bf16[8,2,512,16]{2,3,0,1:T(8,128)(2,1)S(1)} %bitcast.130), kind=kOutput, calls=%fused_computation.3 | convolution fusion | flops 81784832 | bytes 8929280 | tf_op jit(solution)/shard_map/hid,hjd->hij/dot_general | solution.py:100
  44.8 9.0 %collective-permute-start.2 = (f32[8,273]{1,0:T(8,128)S(1)}, f32[8,273]{1,0:T(8,128)S(1)}, u32[]{:S(2)}, u32[]{:S(2)}) collective-permute-start(f32[8,273]{1,0:T(8,128)S(1)} %multiply_add_fusion.5), channel_id=1, source_target_pairs={{0,4},{4,8},{8,12},{12,16},{16,20},{20,24},{24,28},{1,5},{5,9},{9,... | collective-permute-start | bytes 26216 | tf_op jit(solution)/shard_map/ppermute | solution.py:20
  54.1 4.5 %collective-permute-start.6 = (f32[8,273,128]{2,0,1:T(8,128)S(1)}, f32[8,273,128]{2,0,1:T(8,128)S(1)}, u32[]{:S(2)}, u32[]{:S(2)}) collective-permute-start(f32[8,273,128]{2,0,1:T(8,128)S(1)} %multiply_add_fusion.2), channel_id=1, source_target_pairs={{0,4},{4,8},{8,12},{12,16},{16,20},{20,24},{24,28},{1,5},{5,9},{9,... | collective-permute-start | bytes 3354632 | tf_op jit(solution)/shard_map/ppermute | solution.py:20
  58.6 3.3 %fusion.13 = f32[8,512,128]{1,2,0:T(8,128)} fusion(bf16[8,512,128]{2,0,1:T(8,128)(2,1)S(1)} %bitcast.138, f32[8,512,512]{1,2,0:T(8,128)S(1)} %get-tuple-element.33, pred[512,512]{0,1:T(8,128)(4,1)S(1)} %fusion.15), kind=kOutput, calls=%fused_computation.42 | convolution fusion | flops 551550976 | bytes 11796480 | tf_op jit(solution)/shard_map/hij,hjd->hid/dot_general | solution.py:109
  67.1 8.7 %collective-permute-start.7 = (bf16[8,273,128]{2,0,1:T(8,128)(2,1)}, bf16[8,273,128]{2,0,1:T(8,128)(2,1)S(1)}, u32[]{:S(2)}, u32[]{:S(2)}) collective-permute-start(bf16[8,273,128]{2,0,1:T(8,128)(2,1)} %multiply_add_fusion.1), channel_id=1, source_target_pairs={{0,4},{4,8},{8,12},{12,16},{16,20},{20,24},{24,28},{1,5},{5,9},{9,... | collective-permute-start | bytes 1677320 | tf_op jit(solution)/shard_map/ppermute | solution.py:20
  75.8 17.2 %all-gather.2.cloned.1.call-done = bf16[512,4096]{1,0:T(8,128)(2,1)} async-done(((bf16[512,1024]{1,0:T(8,128)(2,1)}), bf16[512,4096]{1,0:T(8,128)(2,1)}) %all-gather.2.cloned.1.call-update) | async-done | bytes 4194320 | tf_op jit(solution)/shard_map/all_gather | solution.py:92
  93.0 8.3 %fusion.47 = f32[512,1024]{0,1:T(8,128)S(1)} fusion(bf16[512,4096]{1,0:T(8,128)(2,1)} %all-gather.2.cloned.1.call-done, bf16[1024,4096]{1,0:T(8,128)(2,1)} %param.8), kind=kOutput, calls=%fused_computation.102 | convolution fusion | flops 4294967296 | bytes 14680064 | tf_op jit(solution)/shard_map/reshape | solution.py:96
  101.5 2.5 %divide_convert_fusion = (bf16[8,512,128]{1,2,0:T(8,128)(2,1)}, f32[8,512]{1,0:T(8,128)S(1)}, f32[8,512,128]{1,2,0:T(8,128)S(1)}) fusion(f32[8,512,128]{1,2,0:T(8,128)S(1)} %bitcast.146, f32[8,512]{1,0:T(8,128)S(1)} %fusion.32, f32[512,1024]{0,1:T(8,128)S(1)} %fusion.47, f32[8,512,128]{1,2,0:T(8,128)S(1)} %copy-done.18, ...), kind=kOutput, calls=%fused_computation.24 | convolution fusion | flops 296636416 | bytes 12259874 | tf_op jit(solution)/shard_map/hif,hfd->hid/dot_general | solution.py:107
  104.2 8.1 %fusion.48 = f32[1024,4096]{1,0:T(8,128)} fusion(bf16[512,1024]{0,1:T(8,128)(2,1)S(1)} %bitcast.137, bf16[512,4096]{1,0:T(8,128)(2,1)S(1)} %copy-done.15), kind=kOutput, calls=%fused_computation.103 | convolution fusion | flops 4294967296 | bytes 22020096 | tf_op jit(solution)/shard_map/dot_general | solution.py:141
  112.4 3.1 %add_convert_fusion.1 = (bf16[8,273,128]{2,1,0:T(8,128)(2,1)S(1)}, f32[8,273,128]{2,1,0:T(8,128)S(1)}) fusion(f32[]{:T(128)S(6)} %mul.252, bf16[8,512,128]{1,2,0:T(8,128)(2,1)} %get-tuple-element.28, pred[512]{0:T(512)(128)(4,1)S(1)} %get-tuple-element.30, bf16[8,512,256]{1,2,0:T(8,128)(2,1)} %bitcast.134, bf16[8,512,16]{1,2,0:T(8,128)(2,1)} %copy-done.12, ...), kind=kOutput, calls=%fused_computation.31 | convolution fusion | flops 294647808 | bytes 4955174 | tf_op jit(solution)/shard_map/hif,hid->hfd/dot_general | solution.py:136
  122.4 3.3 %fusion.44 = f32[8,512,128]{1,2,0:T(8,128)} fusion(bf16[8,512,128]{1,2,0:T(8,128)(2,1)S(1)} %copy-done.7, f32[8,512,512]{1,2,0:T(8,128)S(1)} %bitcast.148, pred[512,512]{0,1:T(8,128)(4,1)S(1)} %copy-done.11), kind=kOutput, calls=%fused_computation.101 | convolution fusion | flops 551550976 | bytes 11796480 | tf_op jit(solution)/shard_map/hij,hid->hjd/dot_general | solution.py:124
  127.5 2.5 %select_convert_fusion = bf16[8,512,512]{1,2,0:T(8,128)(2,1)S(1)} fusion(f32[8,512,512]{1,2,0:T(8,128)S(1)} %bitcast.148, f32[8,512]{1,0:T(8,128)S(1)} %negate_divide_fusion, pred[512,512]{0,1:T(8,128)(4,1)S(1)} %copy-done.11, bf16[8,512,128]{1,2,0:T(8,128)(2,1)S(1)} %copy-done.7, bf16[512,1024]{1,0:T(8,128)(2,1)S(1)} %copy-done.3), kind=kOutput, calls=%fused_computation | convolution fusion | flops 549453824 | bytes 14958592 | tf_op jit(solution)/shard_map/hid,hjd->hij/dot_general | solution.py:120
  130.0 5.4 %collective-permute-done.9 = bf16[8,273,128]{2,0,1:T(8,128)(2,1)S(1)} collective-permute-done((bf16[8,273,128]{2,0,1:T(8,128)(2,1)S(1)}, bf16[8,273,128]{2,0,1:T(8,128)(2,1)S(1)}, u32[]{:S(2)}, u32[]{:S(2)}) %collective-permute-start.9) | collective-permute-done | bytes 559136 | tf_op jit(solution)/shard_map/ppermute | solution.py:20
  138.3 3.6 %fusion.5 = f32[8,512,16]{1,2,0:T(8,128)S(1)} fusion(f32[8,512,16,16]{1,3,2,0:T(8,128)S(1)} %bitcast.122, f32[8,512,16]{1,2,0:T(8,128)S(1)} %get-tuple-element.26), kind=kLoop, calls=%fused_computation.12 | loop fusion | flops 3080192 | bytes 4718592 | tf_op jit(solution)/shard_map/reduce_sum | solution.py:45
  141.9 5.2 %collective-permute-done.13 = bf16[8,273]{1,0:T(8,128)(2,1)S(1)} collective-permute-done((bf16[8,273]{1,0:T(8,128)(2,1)S(1)}, bf16[8,273]{1,0:T(8,128)(2,1)S(1)}, u32[]{:S(2)}, u32[]{:S(2)}) %collective-permute-start.13) | collective-permute-done | bytes 4400 | tf_op jit(solution)/shard_map/ppermute | solution.py:20
  149.9 15.3 %collective-permute-done.14 = bf16[8,273]{1,0:T(8,128)(2,1)S(1)} collective-permute-done((bf16[8,273]{1,0:T(8,128)(2,1)S(1)}, bf16[8,273]{1,0:T(8,128)(2,1)S(1)}, u32[]{:S(2)}, u32[]{:S(2)}) %collective-permute-start.14) | collective-permute-done | bytes 4400 | tf_op jit(solution)/shard_map/ppermute | solution.py:20
  167.4 3.4 %collective-permute-done.15 = bf16[8,273]{1,0:T(8,128)(2,1)S(1)} collective-permute-done((bf16[8,273]{1,0:T(8,128)(2,1)S(1)}, bf16[8,273]{1,0:T(8,128)(2,1)S(1)}, u32[]{:S(2)}, u32[]{:S(2)}) %collective-permute-start.15) | collective-permute-done | bytes 4400 | tf_op jit(solution)/shard_map/ppermute | solution.py:20
  178.1 3.6 %fusion.3 = f32[8,512,16]{1,2,0:T(8,128)S(1)} fusion(f32[8,512,16,16]{1,3,2,0:T(8,128)S(1)} %bitcast.123, f32[8,512,16]{1,2,0:T(8,128)S(1)} %get-tuple-element.27), kind=kLoop, calls=%fused_computation.9 | loop fusion | flops 3080192 | bytes 4718592 | tf_op jit(solution)/shard_map/reduce_sum | solution.py:45
  183.8 54.1 %reduce-scatter.2.cloned.1.call-done = f32[1024,512]{1,0:T(8,128)} async-done(((f32[1024,4096]{1,0:T(8,128)}), f32[1024,512]{1,0:T(8,128)}) %reduce-scatter.2.cloned.1.call-update) | async-done | bytes 2097168 | tf_op jit(solution)/shard_map/reduce_scatter | solution.py:144
  (120 shorter events, 39.9 us)
Async XLA Ops:
  7.2 85.9 %all-gather.2.cloned.1.call-start = ((), (), s32[]{:S(2)}) async-start(), calls=%async_computation.1 | async-start | bytes 5242880 | tf_op jit(solution)/shard_map/all_gather | solution.py:92
  7.9 230.0 %reduce-scatter.2.cloned.1.call-start = ((), (), s32[]{:S(2)}) async-start(), calls=%async_computation.2 | async-start | bytes 18874368 | tf_op jit(solution)/shard_map/reduce_scatter | solution.py:144
  14.0 50.6 %copy-start.12 = (bf16[8,512,16]{1,2,0:T(8,128)(2,1)}, bf16[8,512,16]{1,2,0:T(8,128)(2,1)S(1)}, u32[]{:S(2)}) copy-start(bf16[8,512,16]{1,2,0:T(8,128)(2,1)S(1)} %get-tuple-element.24) | copy-start | bytes 393220
  17.3 8.1 %collective-permute-start.4 = (f32[8,273,128]{2,0,1:T(8,128)S(1)}, f32[8,273,128]{2,0,1:T(8,128)S(1)}, u32[]{:S(2)}, u32[]{:S(2)}) collective-permute-start(f32[8,273,128]{2,0,1:T(8,128)S(1)} %copy.122), channel_id=1, source_target_pairs={{0,4},{4,8},{8,12},{12,16},{16,20},{20,24},{24,28},{1,5},{5,9},{9,... | collective-permute-start | bytes 3354632 | tf_op jit(solution)/shard_map/ppermute | solution.py:20
  20.9 16.3 %collective-permute-start = (f32[8,273]{1,0:T(8,128)S(1)}, f32[8,273]{1,0:T(8,128)S(1)}, u32[]{:S(2)}, u32[]{:S(2)}) collective-permute-start(f32[8,273]{1,0:T(8,128)S(1)} %broadcast_add_fusion.1), channel_id=1, source_target_pairs={{0,4},{4,8},{8,12},{12,16},{16,20},{20,24},{24,28},{1,5},{5,9},{9,... | collective-permute-start | bytes 26216 | tf_op jit(solution)/shard_map/ppermute | solution.py:20
  25.6 28.2 %collective-permute-start.5 = (f32[8,273,128]{2,0,1:T(8,128)S(1)}, f32[8,273,128]{2,0,1:T(8,128)S(1)}, u32[]{:S(2)}, u32[]{:S(2)}) collective-permute-start(f32[8,273,128]{2,0,1:T(8,128)S(1)} %multiply_add_fusion.3), channel_id=1, source_target_pairs={{0,4},{4,8},{8,12},{12,16},{16,20},{20,24},{24,28},{1,5},{5,9},{9,... | collective-permute-start | bytes 3354632 | tf_op jit(solution)/shard_map/ppermute | solution.py:20
  37.2 21.4 %copy-start.10 = (pred[512,512]{0,1:T(8,128)(4,1)}, pred[512,512]{0,1:T(8,128)(4,1)S(1)}, u32[]{:S(2)}) copy-start(pred[512,512]{0,1:T(8,128)(4,1)S(1)} %fusion.15) | copy-start | bytes 786436
  37.2 7.6 %collective-permute-start.1 = (f32[8,273]{1,0:T(8,128)S(1)}, f32[8,273]{1,0:T(8,128)S(1)}, u32[]{:S(2)}, u32[]{:S(2)}) collective-permute-start(f32[8,273]{1,0:T(8,128)S(1)} %multiply_add_fusion.6), channel_id=1, source_target_pairs={{0,4},{4,8},{8,12},{12,16},{16,20},{20,24},{24,28},{1,5},{5,9},{9,... | collective-permute-start | bytes 26216 | tf_op jit(solution)/shard_map/ppermute | solution.py:20
  44.5 17.4 %copy-start.16 = (f32[8,512,512]{1,2,0:T(8,128)}, f32[8,512,512]{1,2,0:T(8,128)S(1)}, u32[]{:S(2)}) copy-start(f32[8,512,512]{1,2,0:T(8,128)S(1)} %get-tuple-element.33) | copy-start | bytes 25165828
  44.8 17.0 %collective-permute-start.2 = (f32[8,273]{1,0:T(8,128)S(1)}, f32[8,273]{1,0:T(8,128)S(1)}, u32[]{:S(2)}, u32[]{:S(2)}) collective-permute-start(f32[8,273]{1,0:T(8,128)S(1)} %multiply_add_fusion.5), channel_id=1, source_target_pairs={{0,4},{4,8},{8,12},{12,16},{16,20},{20,24},{24,28},{1,5},{5,9},{9,... | collective-permute-start | bytes 26216 | tf_op jit(solution)/shard_map/ppermute | solution.py:20
  54.1 11.9 %collective-permute-start.6 = (f32[8,273,128]{2,0,1:T(8,128)S(1)}, f32[8,273,128]{2,0,1:T(8,128)S(1)}, u32[]{:S(2)}, u32[]{:S(2)}) collective-permute-start(f32[8,273,128]{2,0,1:T(8,128)S(1)} %multiply_add_fusion.2), channel_id=1, source_target_pairs={{0,4},{4,8},{8,12},{12,16},{16,20},{20,24},{24,28},{1,5},{5,9},{9,... | collective-permute-start | bytes 3354632 | tf_op jit(solution)/shard_map/ppermute | solution.py:20
  61.9 2.7 %collective-permute-start.3 = (f32[8,273]{1,0:T(8,128)S(1)}, f32[8,273]{1,0:T(8,128)S(1)}, u32[]{:S(2)}, u32[]{:S(2)}) collective-permute-start(f32[8,273]{1,0:T(8,128)S(1)} %multiply_add_fusion.4), channel_id=1, source_target_pairs={{0,4},{4,8},{8,12},{12,16},{16,20},{20,24},{24,28},{1,5},{5,9},{9,... | collective-permute-start | bytes 26216 | tf_op jit(solution)/shard_map/ppermute | solution.py:20
  67.1 34.3 %collective-permute-start.7 = (bf16[8,273,128]{2,0,1:T(8,128)(2,1)}, bf16[8,273,128]{2,0,1:T(8,128)(2,1)S(1)}, u32[]{:S(2)}, u32[]{:S(2)}) collective-permute-start(bf16[8,273,128]{2,0,1:T(8,128)(2,1)} %multiply_add_fusion.1), channel_id=1, source_target_pairs={{0,4},{4,8},{8,12},{12,16},{16,20},{20,24},{24,28},{1,5},{5,9},{9,... | collective-permute-start | bytes 1677320 | tf_op jit(solution)/shard_map/ppermute | solution.py:20
  117.7 19.3 %collective-permute-start.12 = (bf16[8,273]{1,0:T(8,128)(2,1)S(1)}, bf16[8,273]{1,0:T(8,128)(2,1)S(1)}, u32[]{:S(2)}, u32[]{:S(2)}) collective-permute-start(bf16[8,273]{1,0:T(8,128)(2,1)S(1)} %fusion.34), channel_id=1, source_target_pairs={{4,0},{8,4},{12,8},{16,12},{20,16},{24,20},{28,24},{5,1},{9,5},{13... | collective-permute-start | bytes 13112 | tf_op jit(solution)/shard_map/ppermute | solution.py:20
  119.2 6.5 %collective-permute-start.8 = (bf16[8,273,128]{2,0,1:T(8,128)(2,1)S(1)}, bf16[8,273,128]{2,0,1:T(8,128)(2,1)S(1)}, u32[]{:S(2)}, u32[]{:S(2)}) collective-permute-start(bf16[8,273,128]{2,0,1:T(8,128)(2,1)S(1)} %copy.133), channel_id=1, source_target_pairs={{4,0},{8,4},{12,8},{16,12},{20,16},{24,20},{28,24},{5,1},{9,5},{13... | collective-permute-start | bytes 1677320 | tf_op jit(solution)/shard_map/ppermute | solution.py:20
  126.0 9.4 %collective-permute-start.9 = (bf16[8,273,128]{2,0,1:T(8,128)(2,1)S(1)}, bf16[8,273,128]{2,0,1:T(8,128)(2,1)S(1)}, u32[]{:S(2)}, u32[]{:S(2)}) collective-permute-start(bf16[8,273,128]{2,0,1:T(8,128)(2,1)S(1)} %add_convert_fusion.4), channel_id=1, source_target_pairs={{4,0},{8,4},{12,8},{16,12},{20,16},{24,20},{28,24},{5,1},{9,5},{13... | collective-permute-start | bytes 1677320 | tf_op jit(solution)/shard_map/ppermute | solution.py:20
  130.0 36.8 %copy-start = (bf16[8,512,512]{1,2,0:T(8,128)(2,1)}, bf16[8,512,512]{1,2,0:T(8,128)(2,1)S(1)}, u32[]{:S(2)}) copy-start(bf16[8,512,512]{1,2,0:T(8,128)(2,1)S(1)} %select_convert_fusion) | copy-start | bytes 12582916
  135.7 12.7 %collective-permute-start.10 = (bf16[8,273,128]{2,0,1:T(8,128)(2,1)S(1)}, bf16[8,273,128]{2,0,1:T(8,128)(2,1)S(1)}, u32[]{:S(2)}, u32[]{:S(2)}) collective-permute-start(bf16[8,273,128]{2,0,1:T(8,128)(2,1)S(1)} %add_convert_fusion.3), channel_id=1, source_target_pairs={{4,0},{8,4},{12,8},{16,12},{20,16},{24,20},{28,24},{5,1},{9,5},{13... | collective-permute-start | bytes 1677320 | tf_op jit(solution)/shard_map/ppermute | solution.py:20
  137.0 10.1 %collective-permute-start.13 = (bf16[8,273]{1,0:T(8,128)(2,1)S(1)}, bf16[8,273]{1,0:T(8,128)(2,1)S(1)}, u32[]{:S(2)}, u32[]{:S(2)}) collective-permute-start(bf16[8,273]{1,0:T(8,128)(2,1)S(1)} %fusion.35), channel_id=1, source_target_pairs={{4,0},{8,4},{12,8},{16,12},{20,16},{24,20},{28,24},{5,1},{9,5},{13... | collective-permute-start | bytes 13112 | tf_op jit(solution)/shard_map/ppermute | solution.py:20
  141.9 29.0 %copy-start.9 = (bf16[8,512,16]{1,2,0:T(8,128)(2,1)S(1)}, bf16[8,512,16]{1,2,0:T(8,128)(2,1)}, u32[]{:S(2)}) copy-start(bf16[8,512,16]{1,2,0:T(8,128)(2,1)} %copy-done.8) | copy-start | bytes 393220
  141.9 29.0 %copy-start.17 = (f32[8,512,128]{1,2,0:T(8,128)S(1)}, f32[8,512,128]{1,2,0:T(8,128)}, u32[]{:S(2)}) copy-start(f32[8,512,128]{1,2,0:T(8,128)} %fusion.44) | copy-start | bytes 6291460
  147.1 18.1 %collective-permute-start.14 = (bf16[8,273]{1,0:T(8,128)(2,1)S(1)}, bf16[8,273]{1,0:T(8,128)(2,1)S(1)}, u32[]{:S(2)}, u32[]{:S(2)}) collective-permute-start(bf16[8,273]{1,0:T(8,128)(2,1)S(1)} %fusion.36), channel_id=1, source_target_pairs={{4,0},{8,4},{12,8},{16,12},{20,16},{24,20},{28,24},{5,1},{9,5},{13... | collective-permute-start | bytes 13112 | tf_op jit(solution)/shard_map/ppermute | solution.py:20
  148.6 22.2 %collective-permute-start.11 = (bf16[8,273,128]{2,0,1:T(8,128)(2,1)S(1)}, bf16[8,273,128]{2,0,1:T(8,128)(2,1)S(1)}, u32[]{:S(2)}, u32[]{:S(2)}) collective-permute-start(bf16[8,273,128]{2,0,1:T(8,128)(2,1)S(1)} %add_convert_fusion.2), channel_id=1, source_target_pairs={{4,0},{8,4},{12,8},{16,12},{20,16},{24,20},{28,24},{5,1},{9,5},{13... | collective-permute-start | bytes 1677320 | tf_op jit(solution)/shard_map/ppermute | solution.py:20
  165.2 5.6 %collective-permute-start.15 = (bf16[8,273]{1,0:T(8,128)(2,1)S(1)}, bf16[8,273]{1,0:T(8,128)(2,1)S(1)}, u32[]{:S(2)}, u32[]{:S(2)}) collective-permute-start(bf16[8,273]{1,0:T(8,128)(2,1)S(1)} %fusion.37), channel_id=1, source_target_pairs={{4,0},{8,4},{12,8},{16,12},{20,16},{24,20},{28,24},{5,1},{9,5},{13... | collective-permute-start | bytes 13112 | tf_op jit(solution)/shard_map/ppermute | solution.py:20
  (15 other events, 76.1 us)
Sparse Core Ops, SparseCore 0:
  9.5 83.4 all-gather.1
  112.5 125.3 reduce-scatter.1
where the time goes:
time: 245 us
  waiting for transfers between devices  101 us (41%)
  starting transfers between devices  58 us (24%)
  matrix products  46.6 us (19%)
  between operations  16.1 us (7%)
  other arithmetic  14.7 us (6%)
  local copies, waits for them, and re-layouts  7.85 us (3%)
    ppermute x16, starting transfers between devices, shifted(): lax.ppermute(value, axis, [(source, source + steps) for source in range(l...  57.9 us
    reduce_scatter x1, waiting for transfers between devices, on_device(): proj_grad = lax.psum_scatter(term, 'ctx', scatter_dimension=1, tiled=True)  54.1 us
    ppermute x16, waiting for transfers between devices, shifted(): lax.ppermute(value, axis, [(source, source + steps) for source in range(l...  29.5 us
    all_gather x1, waiting for transfers between devices, on_device(): full_out = lax.all_gather(out_grad, 'head', axis=1, tiled=True)  17.2 us
    reshape x1, matrix products, on_device(): grads_out = out_rows.reshape(tokens, head_count, HEAD).transpose(1, 0, 2)  8.35 us
    dot_general x1, matrix products, on_device(): lax.dot_general(attended_all, full_out, (((0,), (0,)), ((), ())), preferr...  8.11 us
    reduce_sum x2, other arithmetic, feature_grad(): return linear + quad_scale * jnp.sum(paired * points[..., None, :], axis=-1)  7.13 us
  transfers between devices with their start and end apart: 18, of which 7 were waited for; matrix products, arithmetic and copies ran while one was open for 24% of the time, Pallas kernels for 0%

commit v1 on v0

v1 whole, which is shorter than its diff:
```python
import math

import jax
import jax.numpy as jnp
import numpy as np
from jax import lax
from jax.sharding import PartitionSpec as P

HEAD = 128
QK = 16
CHIP_SPAN = 2

quad_scale = 0.25 / math.sqrt(2.0)

bf16 = jnp.bfloat16
f32 = jnp.float32

PAIRS = [(a, b) for a in range(QK) for b in range(a, QK)]
KEPT = 1 + QK + len(PAIRS)
FEAT = 160


def tables():
    left = np.zeros((QK, FEAT), np.float32)
    right = np.zeros((QK, FEAT), np.float32)
    left_add = np.zeros((FEAT,), np.float32)
    right_add = np.zeros((FEAT,), np.float32)
    scale = np.zeros((FEAT,), np.float32)
    weight = np.ones((FEAT,), np.float32)
    left_add[0] = right_add[0] = scale[0] = 1.0
    for a in range(QK):
        left[a, 1 + a] = 1.0
        right_add[1 + a] = 1.0
        scale[1 + a] = 0.5
    for place, (a, b) in enumerate(PAIRS):
        left[a, 1 + QK + place] = 1.0
        right[b, 1 + QK + place] = 1.0
        scale[1 + QK + place] = quad_scale
        weight[1 + QK + place] = 1.0 if a == b else 2.0
    return left, right, left_add, right_add, scale, weight


LEFT, RIGHT, LEFT_ADD, RIGHT_ADD, SCALE, WEIGHT = tables()


def dot(spec, a, b):
    return jnp.einsum(spec, a, b, preferred_element_type=f32)


def factors(points):
    first = dot("htd,df->htf", points, jnp.asarray(LEFT, bf16)) + LEFT_ADD
    second = dot("htd,df->htf", points, jnp.asarray(RIGHT, bf16)) + RIGHT_ADD
    return first, second


def feature_grad(grad_feat, first, second):
    scaled = grad_feat * (SCALE * WEIGHT)
    return dot("htf,df->htd", (scaled * second).astype(bf16), jnp.asarray(LEFT, bf16)) + dot(
        "htf,df->htd", (scaled * first).astype(bf16), jnp.asarray(RIGHT, bf16)
    )


def segment_ids(doc_lengths, positions):
    starts = jnp.cumsum(doc_lengths, dtype=jnp.int32) - doc_lengths
    return jnp.sum((starts[None, :] <= positions[:, None]).astype(jnp.int32), axis=1) - 1


def chip_shift(parts, chips, steps):
    moves = [
        (2 * c + core, 2 * (c + steps) + core)
        for c in range(chips)
        for core in range(2)
        if 0 <= c + steps < chips
    ]
    return [lax.ppermute(part, "ctx", moves) for part in parts]


def swap(parts, count):
    return [lax.ppermute(part, "ctx", [(c, c ^ 1) for c in range(count)]) for part in parts]


def carried_in(parts, edges, step, count):
    index = lax.axis_index("ctx")
    core = index % 2
    sent = [parts[0].astype(bf16), parts[1]]
    other = swap(sent, count)
    early = core == (0 if step > 0 else 1)
    near = [jnp.where(early, o, s).astype(f32) for o, s in zip(other, sent)]
    far = [jnp.where(early, s, o).astype(f32) for o, s in zip(other, sent)]
    chip = index // 2

    def keep(block):
        inside = (block >= 0) & (block < count)
        return jnp.where(inside & (edges(block) == edges(block + 1)), 1.0, 0.0)

    near_block = 2 * chip + (1 if step > 0 else 0)
    keep_near = keep(near_block)
    pair = [(n + keep_near * f).astype(s.dtype) for n, f, s in zip(near, far, sent)]
    arrived = [chip_shift(pair, count // 2, step * (k + 1)) for k in range(CHIP_SPAN)]
    total = [a.astype(f32) for a in arrived[0]]
    through = jnp.float32(1.0)
    for k in range(1, CHIP_SPAN):
        base = 2 * (chip - step * k)
        through = through * keep(base) * keep(base + 1)
        total = [t + through * a.astype(f32) for t, a in zip(total, arrived[k])]
    first_kept = keep(2 * chip + (0 if step > 0 else 1))
    late = [f + first_kept * t for f, t in zip(far, total)]
    return [jnp.where(early, t, l) for t, l in zip(total, late)]


def reduce_halves(attended, full_out, count):
    index = lax.axis_index("ctx")
    chip, core = index // 2, index % 2
    chips = count // 2
    width = full_out.shape[1] // count
    rows = attended.shape[1]

    def columns(parity):
        return [
            lax.dynamic_slice_in_dim(full_out, (((r ^ chip) * 2) + parity) * width, width, 1)
            for r in range(chips)
        ]

    def product(picked):
        return lax.dot_general(
            attended,
            jnp.concatenate(picked, axis=1),
            (((0,), (0,)), ((), ())),
            preferred_element_type=f32,
        )

    leaving = product(columns(1 - core)).astype(bf16)
    (came,) = swap([leaving], count)
    mine = product(columns(core)) + came.astype(f32)
    bits = max(1, chips).bit_length() - 1
    half = rows // 2
    flows = []
    for flow, order in ((0, list(range(bits))), (1, list(range(bits))[::-1])):
        held = {
            r: mine[flow * half : (flow + 1) * half, r * width : (r + 1) * width]
            for r in range(chips)
        }
        for bit in order:
            moving = [r for r in held if (r >> bit) & 1]
            packed = jnp.concatenate([held[r].astype(bf16) for r in moving], axis=1)
            got = lax.ppermute(
                packed,
                "ctx",
                [(2 * c + k, 2 * (c ^ (1 << bit)) + k) for c in range(chips) for k in range(2)],
            )
            for place, r in enumerate(moving):
                target = r ^ (1 << bit)
                held[target] = held[target] + got[:, place * width : (place + 1) * width].astype(f32)
                del held[r]
        flows.append(held[0])
    return jnp.concatenate(flows, axis=0)


def on_device(query_key, values, out_grad, out_weight, doc_lengths):
    tokens = query_key.shape[0]
    head_count = out_weight.shape[0] // HEAD
    count = lax.axis_size("ctx")
    depth = lax.axis_size("head")
    level = lax.axis_index("head")
    shard = out_grad.shape[1]
    index = lax.axis_index("ctx")
    offset = index * tokens

    upward, downward, pieces = out_grad, out_grad, [(out_grad, level)]
    for k in range(1, depth):
        upward = lax.ppermute(upward, "head", [(i, i + 1) for i in range(k - 1, depth - 1)])
        downward = lax.ppermute(downward, "head", [(i, i - 1) for i in range(1, depth - k + 1)])
        if 2 * k >= depth:
            pieces.append(
                (
                    jnp.where(level >= k, upward, downward),
                    jnp.where(level >= k, level - k, jnp.minimum(level + k, depth - 1)),
                    (level >= k) | (level + k < depth),
                )
            )
        else:
            pieces.append((upward, jnp.maximum(level - k, 0), level >= k))
            pieces.append((downward, jnp.minimum(level + k, depth - 1), level + k < depth))
    out_rows = jnp.zeros((tokens, out_weight.shape[0]), f32)
    full_out = jnp.zeros((tokens, shard * depth), bf16)
    for piece in pieces:
        part, owner = piece[0], piece[1]
        weight_part = lax.dynamic_slice_in_dim(out_weight, owner * shard, shard, 1)
        out_rows = out_rows + lax.dot_general(
            part, weight_part, (((1,), (1,)), ((), ())), preferred_element_type=f32
        )
        if len(piece) == 3:
            old = lax.dynamic_slice_in_dim(full_out, owner * shard, shard, 1)
            part = jnp.where(piece[2], part, old)
        full_out = lax.dynamic_update_slice_in_dim(full_out, part, owner * shard, 1)

    starts = jnp.cumsum(doc_lengths, dtype=jnp.int32) - doc_lengths

    def edges(block):
        return jnp.sum((starts <= block * tokens - 1).astype(jnp.int32)) - 1

    positions = offset + jnp.arange(tokens, dtype=jnp.int32)
    segment = segment_ids(doc_lengths, positions)
    open_before = edges(index)
    open_after = segment[tokens - 1]
    carried = (segment == open_before).astype(f32)[None, :, None]
    ending = (segment == open_after).astype(f32)[None, :, None]
    paired = query_key.reshape(tokens, head_count, 2, QK).transpose(1, 2, 0, 3)
    queries = paired[:, 0]
    keys_all = paired[:, 1]
    value_rows = values.reshape(tokens, head_count, HEAD).transpose(1, 0, 2)
    query_first, query_second = factors(queries)
    key_first, key_second = factors(keys_all)
    query_feat = (query_first * query_second * SCALE).astype(bf16)
    key_feat = (key_first * key_second * SCALE).astype(bf16)
    ending_feat = jnp.where(ending > 0.5, key_feat, jnp.zeros_like(key_feat))
    state_local = dot("htf,htd->hfd", ending_feat, value_rows)
    norm_local = jnp.sum(ending_feat.astype(f32), axis=1)
    state_in, norm_in = carried_in([state_local, norm_local], edges, 1, count)
    state_b = state_in.astype(bf16)
    query_weighted = query_feat * jnp.asarray(WEIGHT, bf16)
    places = jnp.arange(tokens, dtype=jnp.int32)
    scores = dot("hid,hjd->hij", queries, keys_all) * 0.25
    visible = (places[None, :] <= places[:, None]) & (segment[:, None] == segment[None, :])
    weight = jnp.where(visible[None], 1.0 + scores + 0.5 * scores * scores, 0.0)
    weight_b = weight.astype(bf16)
    from_state = dot("hif,hfd->hid", query_weighted, state_b)
    numerator = dot("hij,hjd->hid", weight_b, value_rows) + carried * from_state
    denominator = (
        jnp.sum(weight, axis=2, keepdims=True)
        + carried
        * jnp.sum(query_weighted.astype(f32) * norm_in[:, None, :], axis=2, keepdims=True)
    )
    attended = numerator / denominator
    attended_all = (
        attended.astype(bf16).transpose(1, 0, 2).reshape(tokens, head_count * HEAD)
    )
    proj_grad = reduce_halves(attended_all, full_out, count)

    grads_out = out_rows.reshape(tokens, head_count, HEAD).transpose(1, 0, 2)
    den_grad = -jnp.sum(grads_out * attended, axis=2, keepdims=True) / denominator
    num_grad = (grads_out / denominator).astype(bf16)
    near_feat = jnp.where(carried > 0.5, query_feat, jnp.zeros_like(query_feat))
    adj_local = dot("hif,hid->hfd", near_feat, num_grad)
    nadj_local = jnp.sum(near_feat.astype(f32) * den_grad, axis=1)
    adj_in, nadj_in = carried_in([adj_local, nadj_local], edges, -1, count)
    adjoint_b = adj_in.astype(bf16)

    mix_grad = dot("hid,hjd->hij", num_grad, value_rows) + den_grad
    score_grad = jnp.where(visible[None], mix_grad * (1.0 + scores), 0.0).astype(bf16)
    value_grad = dot("hij,hid->hjd", weight_b, num_grad)
    key_grad = 0.25 * dot("hij,hid->hjd", score_grad, queries)
    feat_grad = carried * (
        dot("hid,hfd->hif", num_grad, state_b) + den_grad * norm_in[:, None, :]
    )
    query_grad = 0.25 * dot("hij,hjd->hid", score_grad, keys_all) + feature_grad(
        feat_grad, query_first, query_second
    )
    value_grad = value_grad + ending * dot(
        "htf,hfd->htd", key_feat * jnp.asarray(WEIGHT, bf16), adjoint_b
    )
    key_feat_grad = ending * (
        dot("htd,hfd->htf", value_rows, adjoint_b) + nadj_in[:, None, :]
    )
    key_grad = key_grad + feature_grad(key_feat_grad, key_first, key_second)
    qk_grad = (
        jnp.stack([query_grad, key_grad], axis=2)
        .transpose(1, 0, 2, 3)
        .reshape(tokens, head_count * 2 * QK)
        .astype(bf16)
    )
    value_out = (
        value_grad.transpose(1, 0, 2).reshape(tokens, head_count * HEAD).astype(bf16)
    )
    return (qk_grad, value_out, proj_grad)


def solution(mesh):
    placed = (P("ctx", "head"), P("ctx", "head"), P("ctx", "head"), P("head", None), P())
    return jax.shard_map(
        on_device,
        mesh=mesh,
        in_specs=placed,
        out_specs=(P("ctx", "head"), P("ctx", "head"), P("head", "ctx")),
        check_vma=False,
    )
```

time: 245 us -> 240 us (0.980)
  waiting for transfers between devices: 101 us -> 81.7 us
  matrix products: 46.6 us -> 60.4 us
  starting transfers between devices: 58 us -> 44.6 us
  local copies, waits for them, and re-layouts: 7.85 us -> 19.4 us
  other arithmetic: 14.7 us -> 25.1 us
  between operations: 16.1 us -> 7.72 us
    reduce_scatter x1 -> x0, waiting for transfers between devices: 54.1 us -> none  [on_device(): proj_grad = lax.psum_scatter(term, 'ctx', scatter_dimension=1, tiled=True)]
    ppermute x16 -> x23, waiting for transfers between devices: 29.5 us -> 81.7 us  [the longest x3 34.7 us: on_device(): lax.ppermute(downward, 'head', [(i, i - 1) for i in range(1, depth - k +...]
    dot_general x15 -> x27, matrix products: 38.3 us -> 60.4 us  [the longest x20 38.4 us: dot(): return jnp.einsum(spec, a, b, preferred_element_type=f32)]
    all_gather x1 -> x0, waiting for transfers between devices: 17.2 us -> none  [on_device(): full_out = lax.all_gather(out_grad, 'head', axis=1, tiled=True)]
    ppermute x16 -> x23, starting transfers between devices: 57.9 us -> 44.6 us  [the longest x8 16 us: chip_shift(): return [lax.ppermute(part, 'ctx', moves) for part in parts]]
    dynamic_update_slice x0 -> x4, other arithmetic: none -> 12.2 us  [on_device(): full_out = lax.dynamic_update_slice_in_dim(full_out, part, owner * shard, 1)]
    reshape x1 -> x0, matrix products: 8.35 us -> none  [on_device(): grads_out = out_rows.reshape(tokens, head_count, HEAD).transpose(1, 0, 2)]
    unnamed x46 -> x74, local copies, waits for them, and re-layouts: 4.78 us -> 11.9 us
  transfers between devices with their start and end apart: 18 -> 23, of which waited for: 7 -> 7; matrix products, arithmetic and copies ran while one was open for 24% -> 36% of each run, Pallas kernels for 0% -> 0%
where the time goes in v1:
time: 240 us; the launch traced here: 239 us
  waiting for transfers between devices  81.7 us (34%)
  matrix products  60.4 us (25%)
  starting transfers between devices  44.6 us (19%)
  other arithmetic  25.1 us (10%)
  local copies, waits for them, and re-layouts  19.4 us (8%)
  between operations  7.72 us (3%)
    dot_general x20, matrix products, dot(): return jnp.einsum(spec, a, b, preferred_element_type=f32)  38.4 us
    ppermute x3, waiting for transfers between devices, on_device(): lax.ppermute(downward, 'head', [(i, i - 1) for i in range(1, depth - k +...  34.7 us
    ppermute x8, waiting for transfers between devices, chip_shift(): return [lax.ppermute(part, 'ctx', moves) for part in parts]  32.9 us
    ppermute x8, starting transfers between devices, chip_shift(): return [lax.ppermute(part, 'ctx', moves) for part in parts]  16 us
    ppermute x4, starting transfers between devices, reduce_halves(): lax.ppermute(packed, 'ctx', [(2 * c + k, 2 * (c ^ 1 << bit) + k) for c in...  15.9 us
    dot_general x5, matrix products, on_device(): lax.dot_general(part, weight_part, (((1,), (1,)), ((), ())), preferred_el...  14.1 us
    ppermute x4, waiting for transfers between devices, reduce_halves(): lax.ppermute(packed, 'ctx', [(2 * c + k, 2 * (c ^ 1 << bit) + k) for c in...  14 us
    dynamic_update_slice x4, other arithmetic, on_device(): full_out = lax.dynamic_update_slice_in_dim(full_out, part, owner * shard, 1)  12.2 us
  transfers between devices with their start and end apart: 23, of which 7 were waited for; matrix products, arithmetic and copies ran while one was open for 36% of the time, Pallas kernels for 0%

profile of v1, /device:TPU:0, one launch (start us, length us, event | category | flops | bytes accessed | tf_op | source)
XLA Modules:
  0.0 238.9 jit_solution(3474412947356212270)
XLA Ops:
  0.7 6.1 %collective-permute-start = (bf16[512,1024]{1,0:T(8,128)(2,1)}, bf16[512,1024]{1,0:T(8,128)(2,1)}, u32[]{:S(2)}, u32[]{:S(2)}) collective-permute-start(bf16[512,1024]{1,0:T(8,128)(2,1)} %param.22), channel_id=1, source_target_pairs={{0,1},{1,2},{2,3},{4,5},{5,6},{6,7},{8,9},{9,10},{10,11},{12,13},{... | collective-permute-start | bytes 3145736 | tf_op jit(solution)/shard_map/ppermute | solution.py:171
  26.0 6.2 %fusion.1 = (f32[8,512]{1,0:T(8,128)}, f32[8,512,512]{1,2,0:T(8,128)}) fusion(pred[512,512]{0,1:T(8,128)(4,1)} %fusion.82, bf16[8,2,512,16]{2,3,0,1:T(8,128)(2,1)S(1)} %bitcast.170), kind=kOutput, calls=%fused_computation.4 | convolution fusion | flops 81784832 | bytes 8929280 | tf_op jit(solution)/shard_map/hid,hjd->hij/dot_general | solution.py:47
  32.2 4.6 %fusion.37 = f32[1024,512]{1,0:T(8,128)} fusion(bf16[512,1024]{1,0:T(8,128)(2,1)} %param.22, bf16[1024,4096]{1,0:T(8,128)(2,1)} %param.23, s32[]{:T(128)S(6)} %select_n.206), kind=kOutput, calls=%fused_computation.57 | convolution fusion | flops 1073741824 | bytes 5242884 | tf_op jit(solution)/shard_map/dot_general | solution.py:189
  37.7 3.3 %fusion.80 = f32[8,512,128]{1,2,0:T(8,128)} fusion(bf16[8,512,128]{2,0,1:T(8,128)(2,1)S(1)} %bitcast.176, f32[8,512,512]{1,2,0:T(8,128)S(1)} %copy-done.31, pred[512,512]{0,1:T(8,128)(4,1)S(1)} %copy-done.14), kind=kOutput, calls=%fused_computation.90 | convolution fusion | flops 551550976 | bytes 11796480 | tf_op jit(solution)/shard_map/hij,hjd->hid/dot_general | solution.py:47
  47.1 4.0 %collective-permute-start.8 = (f32[8,160]{1,0:T(8,128)}, f32[8,160]{1,0:T(8,128)}, u32[]{:S(2)}, u32[]{:S(2)}) collective-permute-start(f32[8,160]{1,0:T(8,128)} %multiply_add_fusion.3), channel_id=1, source_target_pairs={{0,16},{4,20},{8,24},{12,28},{1,17},{5,21},{9,25},{13,29},{2,18},{... | collective-permute-start | bytes 15368 | tf_op jit(solution)/shard_map/ppermute | solution.py:75
  51.1 4.0 %collective-permute-start.7 = (f32[8,160]{1,0:T(8,128)}, f32[8,160]{1,0:T(8,128)}, u32[]{:S(2)}, u32[]{:S(2)}) collective-permute-start(f32[8,160]{1,0:T(8,128)} %multiply_add_fusion.3), channel_id=1, source_target_pairs={{0,8},{4,12},{8,16},{12,20},{16,24},{20,28},{1,9},{5,13},{9,17},{1... | collective-permute-start | bytes 15368 | tf_op jit(solution)/shard_map/ppermute | solution.py:75
  66.1 10.2 %collective-permute-done.11 = bf16[8,160,128]{2,1,0:T(8,128)(2,1)S(1)} collective-permute-done((bf16[8,160,128]{2,1,0:T(8,128)(2,1)S(1)}, bf16[8,160,128]{2,1,0:T(8,128)(2,1)S(1)}, u32[]{:S(2)}, u32[]{:S(2)}) %collective-permute-start.11) | collective-permute-done | bytes 327712 | tf_op jit(solution)/shard_map/ppermute | solution.py:75
  79.5 3.3 %select_dynamic-update-slice_fusion.3 = bf16[512,4096]{1,0:T(8,128)(2,1)} fusion(bf16[512,4096]{1,0:T(8,128)(2,1)} %constant_dynamic-update-slice_fusion, s32[]{:T(128)S(6)} %select_n.207, bf16[512,1024]{1,0:T(8,128)(2,1)} %collective-permute-done, pred[]{:T(512)S(6)} %ge.41), kind=kLoop, calls=%fused_computation.95 | loop fusion | flops 524288 | bytes 3145733 | tf_op jit(solution)/shard_map/dynamic_update_slice | solution.py:195
  86.3 20.3 %collective-permute-done.3 = bf16[512,1024]{1,0:T(8,128)(2,1)S(1)} collective-permute-done((bf16[512,1024]{1,0:T(8,128)(2,1)}, bf16[512,1024]{1,0:T(8,128)(2,1)S(1)}, u32[]{:S(2)}, u32[]{:S(2)}) %collective-permute-start.3) | collective-permute-done | bytes 1048608 | tf_op jit(solution)/shard_map/ppermute | solution.py:172
  107.9 3.0 %select_dynamic-update-slice_fusion.2 = bf16[512,4096]{1,0:T(8,128)(2,1)} fusion(bf16[512,4096]{1,0:T(8,128)(2,1)} %select_dynamic-update-slice_fusion.3, s32[]{:T(128)S(6)} %select_n.208, bf16[512,1024]{1,0:T(8,128)(2,1)} %collective-permute-done.1, pred[]{:T(512)S(6)} %lt.99), kind=kLoop, calls=%fused_computation.94 | loop fusion | flops 524288 | bytes 3145733 | tf_op jit(solution)/shard_map/dynamic_update_slice | solution.py:195
  113.4 2.9 %select_dynamic-update-slice_fusion.1 = bf16[512,4096]{1,0:T(8,128)(2,1)} fusion(bf16[512,4096]{1,0:T(8,128)(2,1)} %select_dynamic-update-slice_fusion.2, s32[]{:T(128)S(6)} %select_n.212, pred[]{:T(512)S(6)} %or.6, bf16[512,1024]{1,0:T(8,128)(2,1)S(1)} %collective-permute-done.2, bf16[512,1024]{1,0:T(8,128)(2,1)S(1)} %collective-permute-done.3, pred[]{:T(512)S(6)} %ge.33), kind=kLoop, calls=%fused_computation.93 | loop fusion | flops 1048576 | bytes 4194310 | tf_op jit(solution)/shard_map/dynamic_update_slice | solution.py:195
  117.6 14.4 %collective-permute-done.5 = bf16[512,1024]{1,0:T(8,128)(2,1)S(1)} collective-permute-done((bf16[512,1024]{1,0:T(8,128)(2,1)S(1)}, bf16[512,1024]{1,0:T(8,128)(2,1)S(1)}, u32[]{:S(2)}, u32[]{:S(2)}) %collective-permute-start.5) | collective-permute-done | bytes 1048608 | tf_op jit(solution)/shard_map/ppermute | solution.py:172
  132.0 2.9 %select_dynamic-update-slice_fusion = bf16[512,4096]{1,0:T(8,128)(2,1)} fusion(bf16[512,4096]{1,0:T(8,128)(2,1)} %select_dynamic-update-slice_fusion.1, s32[]{:T(128)S(6)} %select_n.216, pred[]{:T(512)S(6)} %or.7, bf16[512,1024]{1,0:T(8,128)(2,1)S(1)} %collective-permute-done.4, bf16[512,1024]{1,0:T(8,128)(2,1)S(1)} %collective-permute-done.5, pred[]{:T(512)S(6)} %ge.34), kind=kLoop, calls=%fused_computation.92 | loop fusion | flops 1048576 | bytes 4194310 | tf_op jit(solution)/shard_map/dynamic_update_slice | solution.py:195
  137.4 4.3 %convolution_convert_fusion = bf16[1024,2048]{1,0:T(8,128)(2,1)} fusion(bf16[512,1024]{0,1:T(8,128)(2,1)S(1)} %bitcast.174, bf16[512,512]{1,0:T(8,128)(2,1)S(1)} %get-tuple-element.36, bf16[512,512]{1,0:T(8,128)(2,1)S(1)} %get-tuple-element.37, bf16[512,512]{1,0:T(8,128)(2,1)S(1)} %get-tuple-element.38, bf16[512,512]{1,0:T(8,128)(2,1)S(1)} %get-tuple-element.39), kind=kOutput, calls=%fused_computation.5 | convolution fusion | flops 2157969408 | bytes 7340032 | tf_op jit(solution)/shard_map/dot_general | solution.py:125
  141.7 3.2 %fusion.28 = f32[512,1024]{0,1:T(8,128)S(1)} fusion(f32[512,1024]{0,1:T(8,128)S(1)} %fusion.31, f32[1024,512]{1,0:T(8,128)S(1)} %fusion.33, f32[1024,512]{1,0:T(8,128)S(1)} %copy-done.9, f32[1024,512]{1,0:T(8,128)S(1)} %fusion.35, bf16[1024,4096]{1,0:T(8,128)(2,1)} %param.23, s32[]{:T(128)S(6)} %select_n.216, ...), kind=kOutput, calls=%fused_computation.44 | convolution fusion | flops 1076363264 | bytes 14680069 | tf_op jit(solution)/shard_map/dot_general | solution.py:189
  148.4 4.7 %select_convert_fusion = bf16[8,512,512]{1,2,0:T(8,128)(2,1)S(1)} fusion(f32[8,512,512]{1,2,0:T(8,128)} %get-tuple-element.48, f32[8,512]{1,0:T(8,128)S(1)} %negate_divide_fusion, pred[512,512]{0,1:T(8,128)(4,1)S(1)} %copy-done.15, bf16[8,512,128]{1,2,0:T(8,128)(2,1)S(1)} %get-tuple-element.43, bf16[512,1024]{1,0:T(8,128)(2,1)S(1)} %copy-done.8), kind=kOutput, calls=%fused_computation.1 | convolution fusion | flops 549453824 | bytes 14958592 | tf_op jit(solution)/shard_map/hid,hjd->hij/dot_general | solution.py:47
  155.6 4.6 %fusion.122 = f32[8,512,128]{1,2,0:T(8,128)S(1)} fusion(bf16[8,512,128]{1,2,0:T(8,128)(2,1)S(1)} %get-tuple-element.43, f32[8,512,512]{1,2,0:T(8,128)} %get-tuple-element.48, pred[512,512]{0,1:T(8,128)(4,1)S(1)} %copy-done.15), kind=kOutput, calls=%fused_computation.183 | convolution fusion | flops 551550976 | bytes 11796480 | tf_op jit(solution)/shard_map/hij,hid->hjd/dot_general | solution.py:47
  163.7 3.7 %fusion.128 = (bf16[1024,2048]{1,0:T(8,128)(2,1)S(1)}, f32[1024,2048]{1,0:T(8,128)S(1)}) fusion(bf16[1024,2048]{1,0:T(8,128)(2,1)S(1)} %collective-permute-done.18, bf16[512,1024]{0,1:T(8,128)(2,1)} %bitcast.175, bf16[512,512]{1,0:T(8,128)(2,1)S(1)} %get-tuple-element.40, bf16[512,512]{1,0:T(8,128)(2,1)S(1)} %get-tuple-element.41, ...), kind=kOutput, calls=%fused_computation.185 | convolution fusion | flops 2162163712 | bytes 19922944 | tf_op jit(solution)/shard_map/dot_general | solution.py:125
  174.4 3.4 %collective-permute-start.21 = (bf16[512,1024]{1,0:T(8,128)(2,1)S(1)}, bf16[512,1024]{1,0:T(8,128)(2,1)S(1)}, u32[]{:S(2)}, u32[]{:S(2)}) collective-permute-start(bf16[512,1024]{1,0:T(8,128)(2,1)S(1)} %slice.74), channel_id=1, source_target_pairs={{0,16},{4,20},{8,24},{12,28},{16,0},{20,4},{24,8},{28,12},{1,17},{... | collective-permute-start | bytes 3145736 | tf_op jit(solution)/shard_map/ppermute | solution.py:146
  177.8 5.2 %collective-permute-done.14 = bf16[8,160,128]{2,1,0:T(8,128)(2,1)S(1)} collective-permute-done((bf16[8,160,128]{2,1,0:T(8,128)(2,1)S(1)}, bf16[8,160,128]{2,1,0:T(8,128)(2,1)S(1)}, u32[]{:S(2)}, u32[]{:S(2)}) %collective-permute-start.14) | collective-permute-done | bytes 327712 | tf_op jit(solution)/shard_map/ppermute | solution.py:75
  183.0 17.5 %collective-permute-done.13 = bf16[8,160,128]{2,1,0:T(8,128)(2,1)S(1)} collective-permute-done((bf16[8,160,128]{2,1,0:T(8,128)(2,1)S(1)}, bf16[8,160,128]{2,1,0:T(8,128)(2,1)S(1)}, u32[]{:S(2)}, u32[]{:S(2)}) %collective-permute-start.13) | collective-permute-done | bytes 327712 | tf_op jit(solution)/shard_map/ppermute | solution.py:75
  205.5 9.8 %collective-permute-done.20 = bf16[512,512]{1,0:T(8,128)(2,1)S(1)} collective-permute-done((bf16[512,512]{1,0:T(8,128)(2,1)S(1)}, bf16[512,512]{1,0:T(8,128)(2,1)S(1)}, u32[]{:S(2)}, u32[]{:S(2)}) %collective-permute-start.20) | collective-permute-done | bytes 524320 | tf_op jit(solution)/shard_map/ppermute | solution.py:146
  216.9 7.3 %collective-permute-start.22 = (bf16[512,512]{1,0:T(8,128)(2,1)}, bf16[512,512]{1,0:T(8,128)(2,1)}, u32[]{:S(2)}, u32[]{:S(2)}) collective-permute-start(bf16[512,512]{1,0:T(8,128)(2,1)} %get-tuple-element.32), channel_id=1, source_target_pairs={{0,8},{4,12},{8,0},{12,4},{16,24},{20,28},{24,16},{28,20},{1,9},{5... | collective-permute-start | bytes 1572872 | tf_op jit(solution)/shard_map/ppermute | solution.py:146
  231.4 4.2 %collective-permute-done.22 = bf16[512,512]{1,0:T(8,128)(2,1)} collective-permute-done((bf16[512,512]{1,0:T(8,128)(2,1)}, bf16[512,512]{1,0:T(8,128)(2,1)}, u32[]{:S(2)}, u32[]{:S(2)}) %collective-permute-start.22) | collective-permute-done | bytes 524320 | tf_op jit(solution)/shard_map/ppermute | solution.py:146
  (163 shorter events, 78.0 us)
Async XLA Ops:
  0.7 75.8 %collective-permute-start = (bf16[512,1024]{1,0:T(8,128)(2,1)}, bf16[512,1024]{1,0:T(8,128)(2,1)}, u32[]{:S(2)}, u32[]{:S(2)}) collective-permute-start(bf16[512,1024]{1,0:T(8,128)(2,1)} %param.22), channel_id=1, source_target_pairs={{0,1},{1,2},{2,3},{4,5},{5,6},{6,7},{8,9},{9,10},{10,11},{12,13},{... | collective-permute-start | bytes 3145736 | tf_op jit(solution)/shard_map/ppermute | solution.py:171
  6.8 70.6 %collective-permute-start.1 = (bf16[512,1024]{1,0:T(8,128)(2,1)}, bf16[512,1024]{1,0:T(8,128)(2,1)}, u32[]{:S(2)}, u32[]{:S(2)}) collective-permute-start(bf16[512,1024]{1,0:T(8,128)(2,1)} %param.22), channel_id=1, source_target_pairs={{1,0},{2,1},{3,2},{5,4},{6,5},{7,6},{9,8},{10,9},{11,10},{13,12},{... | collective-permute-start | bytes 3145736 | tf_op jit(solution)/shard_map/ppermute | solution.py:172
  18.9 26.8 %collective-permute-start.6 = (f32[8,160]{1,0:T(8,128)}, f32[8,160]{1,0:T(8,128)}, u32[]{:S(2)}, u32[]{:S(2)}) collective-permute-start(f32[8,160]{1,0:T(8,128)} %get-tuple-element.27), channel_id=1, source_target_pairs={{0,4},{4,0},{8,12},{12,8},{16,20},{20,16},{24,28},{28,24},{1,5},{5... | collective-permute-start | bytes 15368 | tf_op jit(solution)/shard_map/ppermute | solution.py:79
  20.5 39.8 %collective-permute-start.9 = (bf16[8,160,128]{2,1,0:T(8,128)(2,1)S(1)}, bf16[8,160,128]{2,1,0:T(8,128)(2,1)S(1)}, u32[]{:S(2)}, u32[]{:S(2)}) collective-permute-start(bf16[8,160,128]{2,1,0:T(8,128)(2,1)S(1)} %convolution_convert_fusion.2), channel_id=1, source_target_pairs={{0,4},{4,0},{8,12},{12,8},{16,20},{20,16},{24,28},{28,24},{1,5},{5... | collective-permute-start | bytes 983048 | tf_op jit(solution)/shard_map/ppermute | solution.py:79
  47.1 12.4 %collective-permute-start.8 = (f32[8,160]{1,0:T(8,128)}, f32[8,160]{1,0:T(8,128)}, u32[]{:S(2)}, u32[]{:S(2)}) collective-permute-start(f32[8,160]{1,0:T(8,128)} %multiply_add_fusion.3), channel_id=1, source_target_pairs={{0,16},{4,20},{8,24},{12,28},{1,17},{5,21},{9,25},{13,29},{2,18},{... | collective-permute-start | bytes 15368 | tf_op jit(solution)/shard_map/ppermute | solution.py:75
  51.1 8.4 %collective-permute-start.7 = (f32[8,160]{1,0:T(8,128)}, f32[8,160]{1,0:T(8,128)}, u32[]{:S(2)}, u32[]{:S(2)}) collective-permute-start(f32[8,160]{1,0:T(8,128)} %multiply_add_fusion.3), channel_id=1, source_target_pairs={{0,8},{4,12},{8,16},{12,20},{16,24},{20,28},{1,9},{5,13},{9,17},{1... | collective-permute-start | bytes 15368 | tf_op jit(solution)/shard_map/ppermute | solution.py:75
  60.5 15.8 %collective-permute-start.11 = (bf16[8,160,128]{2,1,0:T(8,128)(2,1)S(1)}, bf16[8,160,128]{2,1,0:T(8,128)(2,1)S(1)}, u32[]{:S(2)}, u32[]{:S(2)}) collective-permute-start(bf16[8,160,128]{2,1,0:T(8,128)(2,1)S(1)} %fusion.87), channel_id=1, source_target_pairs={{0,16},{4,20},{8,24},{12,28},{1,17},{5,21},{9,25},{13,29},{2,18},{... | collective-permute-start | bytes 983048 | tf_op jit(solution)/shard_map/ppermute | solution.py:75
  61.9 14.3 %collective-permute-start.10 = (bf16[8,160,128]{2,1,0:T(8,128)(2,1)S(1)}, bf16[8,160,128]{2,1,0:T(8,128)(2,1)S(1)}, u32[]{:S(2)}, u32[]{:S(2)}) collective-permute-start(bf16[8,160,128]{2,1,0:T(8,128)(2,1)S(1)} %fusion.87), channel_id=1, source_target_pairs={{0,8},{4,12},{8,16},{12,20},{16,24},{20,28},{1,9},{5,13},{9,17},{1... | collective-permute-start | bytes 983048 | tf_op jit(solution)/shard_map/ppermute | solution.py:75
  76.5 8.9 %collective-permute-start.2 = (bf16[512,1024]{1,0:T(8,128)(2,1)}, bf16[512,1024]{1,0:T(8,128)(2,1)S(1)}, u32[]{:S(2)}, u32[]{:S(2)}) collective-permute-start(bf16[512,1024]{1,0:T(8,128)(2,1)} %collective-permute-done), channel_id=1, source_target_pairs={{1,2},{2,3},{5,6},{6,7},{9,10},{10,11},{13,14},{14,15},{17,18},{18... | collective-permute-start | bytes 3145736 | tf_op jit(solution)/shard_map/ppermute | solution.py:171
  77.4 29.2 %collective-permute-start.3 = (bf16[512,1024]{1,0:T(8,128)(2,1)}, bf16[512,1024]{1,0:T(8,128)(2,1)S(1)}, u32[]{:S(2)}, u32[]{:S(2)}) collective-permute-start(bf16[512,1024]{1,0:T(8,128)(2,1)} %collective-permute-done.1), channel_id=1, source_target_pairs={{1,0},{2,1},{5,4},{6,5},{9,8},{10,9},{13,12},{14,13},{17,16},{18,1... | collective-permute-start | bytes 3145736 | tf_op jit(solution)/shard_map/ppermute | solution.py:172
  79.5 57.9 %copy-start.10 = (bf16[512,8,128]{0,2,1:T(8,128)(2,1)}, bf16[512,8,128]{0,2,1:T(8,128)(2,1)S(1)}, u32[]{:S(2)}) copy-start(bf16[512,8,128]{0,2,1:T(8,128)(2,1)S(1)} %get-tuple-element.51) | copy-start | bytes 3145732
  85.4 32.2 %collective-permute-start.4 = (bf16[512,1024]{1,0:T(8,128)(2,1)S(1)}, bf16[512,1024]{1,0:T(8,128)(2,1)S(1)}, u32[]{:S(2)}, u32[]{:S(2)}) collective-permute-start(bf16[512,1024]{1,0:T(8,128)(2,1)S(1)} %collective-permute-done.2), channel_id=1, source_target_pairs={{2,3},{6,7},{10,11},{14,15},{18,19},{22,23},{26,27},{30,31}} | collective-permute-start | bytes 3145736 | tf_op jit(solution)/shard_map/ppermute | solution.py:171
  106.6 25.4 %collective-permute-start.5 = (bf16[512,1024]{1,0:T(8,128)(2,1)S(1)}, bf16[512,1024]{1,0:T(8,128)(2,1)S(1)}, u32[]{:S(2)}, u32[]{:S(2)}) collective-permute-start(bf16[512,1024]{1,0:T(8,128)(2,1)S(1)} %collective-permute-done.3), channel_id=1, source_target_pairs={{1,0},{5,4},{9,8},{13,12},{17,16},{21,20},{25,24},{29,28}} | collective-permute-start | bytes 3145736 | tf_op jit(solution)/shard_map/ppermute | solution.py:172
  141.7 22.0 %collective-permute-start.18 = (bf16[1024,2048]{1,0:T(8,128)(2,1)}, bf16[1024,2048]{1,0:T(8,128)(2,1)S(1)}, u32[]{:S(2)}, u32[]{:S(2)}) collective-permute-start(bf16[1024,2048]{1,0:T(8,128)(2,1)} %convolution_convert_fusion), channel_id=1, source_target_pairs={{0,4},{4,0},{8,12},{12,8},{16,20},{20,16},{24,28},{28,24},{1,5},{5... | collective-permute-start | bytes 12582920 | tf_op jit(solution)/shard_map/ppermute | solution.py:79
  146.0 15.1 %collective-permute-start.15 = (f32[8,160]{1,0:T(8,128)S(1)}, f32[8,160]{1,0:T(8,128)S(1)}, u32[]{:S(2)}, u32[]{:S(2)}) collective-permute-start(f32[8,160]{1,0:T(8,128)S(1)} %multiply_reduce_fusion), channel_id=1, source_target_pairs={{0,4},{4,0},{8,12},{12,8},{16,20},{20,16},{24,28},{28,24},{1,5},{5... | collective-permute-start | bytes 15368 | tf_op jit(solution)/shard_map/ppermute | solution.py:79
  147.1 23.2 %collective-permute-start.12 = (bf16[8,160,128]{2,1,0:T(8,128)(2,1)S(1)}, bf16[8,160,128]{2,1,0:T(8,128)(2,1)S(1)}, u32[]{:S(2)}, u32[]{:S(2)}) collective-permute-start(bf16[8,160,128]{2,1,0:T(8,128)(2,1)S(1)} %convolution_convert_fusion.1), channel_id=1, source_target_pairs={{0,4},{4,0},{8,12},{12,8},{16,20},{20,16},{24,28},{28,24},{1,5},{5... | collective-permute-start | bytes 983048 | tf_op jit(solution)/shard_map/ppermute | solution.py:79
  161.1 13.2 %collective-permute-start.17 = (f32[8,160]{1,0:T(8,128)S(1)}, f32[8,160]{1,0:T(8,128)S(1)}, u32[]{:S(2)}, u32[]{:S(2)}) collective-permute-start(f32[8,160]{1,0:T(8,128)S(1)} %multiply_add_fusion.2), channel_id=1, source_target_pairs={{16,0},{20,4},{24,8},{28,12},{17,1},{21,5},{25,9},{29,13},{18,2},{... | collective-permute-start | bytes 15368 | tf_op jit(solution)/shard_map/ppermute | solution.py:75
  162.4 11.9 %collective-permute-start.16 = (f32[8,160]{1,0:T(8,128)S(1)}, f32[8,160]{1,0:T(8,128)S(1)}, u32[]{:S(2)}, u32[]{:S(2)}) collective-permute-start(f32[8,160]{1,0:T(8,128)S(1)} %multiply_add_fusion.2), channel_id=1, source_target_pairs={{8,0},{12,4},{16,8},{20,12},{24,16},{28,20},{9,1},{13,5},{17,9},{2... | collective-permute-start | bytes 15368 | tf_op jit(solution)/shard_map/ppermute | solution.py:75
  167.6 33.1 %collective-permute-start.19 = (bf16[512,1024]{1,0:T(8,128)(2,1)S(1)}, bf16[512,1024]{1,0:T(8,128)(2,1)S(1)}, u32[]{:S(2)}, u32[]{:S(2)}) collective-permute-start(bf16[512,1024]{1,0:T(8,128)(2,1)S(1)} %pad_maximum_fusion.1), channel_id=1, source_target_pairs={{0,8},{4,12},{8,0},{12,4},{16,24},{20,28},{24,16},{28,20},{1,9},{5... | collective-permute-start | bytes 3145736 | tf_op jit(solution)/shard_map/ppermute | solution.py:146
  170.5 12.5 %collective-permute-start.14 = (bf16[8,160,128]{2,1,0:T(8,128)(2,1)S(1)}, bf16[8,160,128]{2,1,0:T(8,128)(2,1)S(1)}, u32[]{:S(2)}, u32[]{:S(2)}) collective-permute-start(bf16[8,160,128]{2,1,0:T(8,128)(2,1)S(1)} %fusion.91), channel_id=1, source_target_pairs={{16,0},{20,4},{24,8},{28,12},{17,1},{21,5},{25,9},{29,13},{18,2},{... | collective-permute-start | bytes 983048 | tf_op jit(solution)/shard_map/ppermute | solution.py:75
  171.8 28.7 %collective-permute-start.13 = (bf16[8,160,128]{2,1,0:T(8,128)(2,1)S(1)}, bf16[8,160,128]{2,1,0:T(8,128)(2,1)S(1)}, u32[]{:S(2)}, u32[]{:S(2)}) collective-permute-start(bf16[8,160,128]{2,1,0:T(8,128)(2,1)S(1)} %fusion.91), channel_id=1, source_target_pairs={{8,0},{12,4},{16,8},{20,12},{24,16},{28,20},{9,1},{13,5},{17,9},{2... | collective-permute-start | bytes 983048 | tf_op jit(solution)/shard_map/ppermute | solution.py:75
  174.4 31.1 %collective-permute-start.21 = (bf16[512,1024]{1,0:T(8,128)(2,1)S(1)}, bf16[512,1024]{1,0:T(8,128)(2,1)S(1)}, u32[]{:S(2)}, u32[]{:S(2)}) collective-permute-start(bf16[512,1024]{1,0:T(8,128)(2,1)S(1)} %slice.74), channel_id=1, source_target_pairs={{0,16},{4,20},{8,24},{12,28},{16,0},{20,4},{24,8},{28,12},{1,17},{... | collective-permute-start | bytes 3145736 | tf_op jit(solution)/shard_map/ppermute | solution.py:146
  200.9 14.4 %collective-permute-start.20 = (bf16[512,512]{1,0:T(8,128)(2,1)S(1)}, bf16[512,512]{1,0:T(8,128)(2,1)S(1)}, u32[]{:S(2)}, u32[]{:S(2)}) collective-permute-start(bf16[512,512]{1,0:T(8,128)(2,1)S(1)} %fusion.78), channel_id=1, source_target_pairs={{0,16},{4,20},{8,24},{12,28},{16,0},{20,4},{24,8},{28,12},{1,17},{... | collective-permute-start | bytes 1572872 | tf_op jit(solution)/shard_map/ppermute | solution.py:146
  216.9 18.8 %collective-permute-start.22 = (bf16[512,512]{1,0:T(8,128)(2,1)}, bf16[512,512]{1,0:T(8,128)(2,1)}, u32[]{:S(2)}, u32[]{:S(2)}) collective-permute-start(bf16[512,512]{1,0:T(8,128)(2,1)} %get-tuple-element.32), channel_id=1, source_target_pairs={{0,8},{4,12},{8,0},{12,4},{16,24},{20,28},{24,16},{28,20},{1,9},{5... | collective-permute-start | bytes 1572872 | tf_op jit(solution)/shard_map/ppermute | solution.py:146
  (34 other events, 265.5 us)

commit v2 on v1

--- a/solution.py
+++ b/solution.py
@@ -9,6 +9,7 @@
 HEAD = 128
 QK = 16
 CHIP_SPAN = 2
+CHUNK = 256
 
 quad_scale = 0.25 / math.sqrt(2.0)
 
@@ -65,47 +66,57 @@
     return jnp.sum((starts[None, :] <= positions[:, None]).astype(jnp.int32), axis=1) - 1
 
 
-def chip_shift(parts, chips, steps):
+def chip_shift(part, chips, steps):
     moves = [
         (2 * c + core, 2 * (c + steps) + core)
         for c in range(chips)
         for core in range(2)
         if 0 <= c + steps < chips
     ]
-    return [lax.ppermute(part, "ctx", moves) for part in parts]
-
-
-def swap(parts, count):
-    return [lax.ppermute(part, "ctx", [(c, c ^ 1) for c in range(count)]) for part in parts]
-
-
-def carried_in(parts, edges, step, count):
+    return lax.ppermute(part, "ctx", moves)
+
+
+def joined(state, norm):
+    half = norm.shape[1] // 2
+    high = norm.astype(bf16).astype(f32)
+    low = norm - high
+    rows = jnp.stack([high[:, :half], high[:, half:], low[:, :half], low[:, half:]], axis=1)
+    rows = jnp.pad(rows, ((0, 0), (KEPT, FEAT - KEPT - 4), (0, HEAD - half)))
+    return (state + rows).astype(bf16)
+
+
+def parted(packed):
+    half = FEAT // 2
+    rows = packed[:, KEPT : KEPT + 4, :half].astype(f32)
+    norm = jnp.concatenate([rows[:, 0] + rows[:, 2], rows[:, 1] + rows[:, 3]], axis=1)
+    inside = (jnp.arange(FEAT) < KEPT)[None, :, None]
+    return jnp.where(inside, packed.astype(f32), 0.0), norm
+
+
+def carried_in(sent, edges, step, count):
     index = lax.axis_index("ctx")
     core = index % 2
-    sent = [parts[0].astype(bf16), parts[1]]
-    other = swap(sent, count)
+    other = lax.ppermute(sent, "ctx", [(c, c ^ 1) for c in range(count)])
     early = core == (0 if step > 0 else 1)
-    near = [jnp.where(early, o, s).astype(f32) for o, s in zip(other, sent)]
-    far = [jnp.where(early, s, o).astype(f32) for o, s in zip(other, sent)]
+    near = parted(jnp.where(early, other, sent))
+    far = parted(jnp.where(early, sent, other))
     chip = index // 2
 
     def keep(block):
         inside = (block >= 0) & (block < count)
         return jnp.where(inside & (edges(block) == edges(block + 1)), 1.0, 0.0)
 
-    near_block = 2 * chip + (1 if step > 0 else 0)
-    keep_near = keep(near_block)
-    pair = [(n + keep_near * f).astype(s.dtype) for n, f, s in zip(near, far, sent)]
-    arrived = [chip_shift(pair, count // 2, step * (k + 1)) for k in range(CHIP_SPAN)]
-    total = [a.astype(f32) for a in arrived[0]]
+    keep_near = keep(2 * chip + (1 if step > 0 else 0))
+    pair = joined(*[n + keep_near * f for n, f in zip(near, far)])
+    arrived = [parted(chip_shift(pair, count // 2, step * (k + 1))) for k in range(CHIP_SPAN)]
+    total = list(arrived[0])
     through = jnp.float32(1.0)
     for k in range(1, CHIP_SPAN):
         base = 2 * (chip - step * k)
         through = through * keep(base) * keep(base + 1)
-        total = [t + through * a.astype(f32) for t, a in zip(total, arrived[k])]
+        total = [t + through * a for t, a in zip(total, arrived[k])]
     first_kept = keep(2 * chip + (0 if step > 0 else 1))
-    late = [f + first_kept * t for f, t in zip(far, total)]
-    return [jnp.where(early, t, l) for t, l in zip(total, late)]
+    return [jnp.where(early, t, f + first_kept * t) for f, t in zip(far, total)]
 
 
 def reduce_halves(attended, full_out, count):
@@ -130,7 +141,7 @@
         )
 
     leaving = product(columns(1 - core)).astype(bf16)
-    (came,) = swap([leaving], count)
+    came = lax.ppermute(leaving, "ctx", [(c, c ^ 1) for c in range(count)])
     mine = product(columns(core)) + came.astype(f32)
     bits = max(1, chips).bit_length() - 1
     half = rows // 2
@@ -161,38 +172,22 @@
     head_count = out_weight.shape[0] // HEAD
     count = lax.axis_size("ctx")
     depth = lax.axis_size("head")
-    level = lax.axis_index("head")
     shard = out_grad.shape[1]
     index = lax.axis_index("ctx")
     offset = index * tokens
 
-    upward, downward, pieces = out_grad, out_grad, [(out_grad, level)]
-    for k in range(1, depth):
-        upward = lax.ppermute(upward, "head", [(i, i + 1) for i in range(k - 1, depth - 1)])
-        downward = lax.ppermute(downward, "head", [(i, i - 1) for i in range(1, depth - k + 1)])
-        if 2 * k >= depth:
-            pieces.append(
-                (
-                    jnp.where(level >= k, upward, downward),
-                    jnp.where(level >= k, level - k, jnp.minimum(level + k, depth - 1)),
-                    (level >= k) | (level + k < depth),
-                )
-            )
-        else:
-            pieces.append((upward, jnp.maximum(level - k, 0), level >= k))
-            pieces.append((downward, jnp.minimum(level + k, depth - 1), level + k < depth))
-    out_rows = jnp.zeros((tokens, out_weight.shape[0]), f32)
-    full_out = jnp.zeros((tokens, shard * depth), bf16)
-    for piece in pieces:
-        part, owner = piece[0], piece[1]
-        weight_part = lax.dynamic_slice_in_dim(out_weight, owner * shard, shard, 1)
-        out_rows = out_rows + lax.dot_general(
-            part, weight_part, (((1,), (1,)), ((), ())), preferred_element_type=f32
+    owners = count // depth
+    width = shard // owners
+    chunks = max(1, width // CHUNK)
+    sub = width // chunks
+    cut = out_grad.reshape(tokens, owners, chunks, sub)
+    cut_weight = out_weight.reshape(-1, count, chunks, sub)
+    gathered, out_rows, proj_parts = [], 0.0, []
+    for h in range(chunks):
+        whole = lax.all_gather(
+            cut[:, :, h].reshape(tokens, owners * sub), "head", axis=1, tiled=True
         )
-        if len(piece) == 3:
-            old = lax.dynamic_slice_in_dim(full_out, owner * shard, shard, 1)
-            part = jnp.where(piece[2], part, old)
-        full_out = lax.dynamic_update_slice_in_dim(full_out, part, owner * shard, 1)
+        gathered.append(whole)
 
     starts = jnp.cumsum(doc_lengths, dtype=jnp.int32) - doc_lengths
 
@@ -216,7 +211,7 @@
     ending_feat = jnp.where(ending > 0.5, key_feat, jnp.zeros_like(key_feat))
     state_local = dot("htf,htd->hfd", ending_feat, value_rows)
     norm_local = jnp.sum(ending_feat.astype(f32), axis=1)
-    state_in, norm_in = carried_in([state_local, norm_local], edges, 1, count)
+    state_in, norm_in = carried_in(joined(state_local, norm_local), edges, 1, count)
     state_b = state_in.astype(bf16)
     query_weighted = query_feat * jnp.asarray(WEIGHT, bf16)
     places = jnp.arange(tokens, dtype=jnp.int32)
@@ -235,7 +230,18 @@
     attended_all = (
         attended.astype(bf16).transpose(1, 0, 2).reshape(tokens, head_count * HEAD)
     )
-    proj_grad = reduce_halves(attended_all, full_out, count)
+    for h, whole in enumerate(gathered):
+        if h > 0:
+            whole, proj_parts[-1] = lax.optimization_barrier((whole, proj_parts[-1]))
+            gathered[h] = whole
+        out_rows = out_rows + lax.dot_general(
+            whole,
+            cut_weight[:, :, h].reshape(-1, count * sub),
+            (((1,), (1,)), ((), ())),
+            preferred_element_type=f32,
+        )
+        if h < chunks - 1:
+            proj_parts.append(reduce_halves(attended_all, whole, count))
 
     grads_out = out_rows.reshape(tokens, head_count, HEAD).transpose(1, 0, 2)
     den_grad = -jnp.sum(grads_out * attended, axis=2, keepdims=True) / denominator
@@ -243,7 +249,10 @@
     near_feat = jnp.where(carried > 0.5, query_feat, jnp.zeros_like(query_feat))
     adj_local = dot("hif,hid->hfd", near_feat, num_grad)
     nadj_local = jnp.sum(near_feat.astype(f32) * den_grad, axis=1)
-    adj_in, nadj_in = carried_in([adj_local, nadj_local], edges, -1, count)
+    adj_sent, last = lax.optimization_barrier((joined(adj_local, nadj_local), gathered[-1]))
+    adj_in, nadj_in = carried_in(adj_sent, edges, -1, count)
+    proj_parts.append(reduce_halves(attended_all, last, count))
+    proj_grad = jnp.concatenate(proj_parts, axis=1)
     adjoint_b = adj_in.astype(bf16)
 
     mix_grad = dot("hid,hjd->hij", num_grad, value_rows) + den_grad

time: 240 us -> 219 us (0.912)
  waiting for transfers between devices: 81.7 us -> 49.9 us
  local copies, waits for them, and re-layouts: 19.4 us -> 41.8 us
  starting transfers between devices: 44.6 us -> 24 us
  between operations: 7.72 us -> 21.3 us
  other arithmetic: 25.1 us -> 22.3 us
    ppermute x19 -> x8, waiting for transfers between devices: 67.6 us -> 22.5 us  [the longest x4 18.1 us: chip_shift(): return lax.ppermute(part, 'ctx', moves)]
    ppermute x19 -> x8, starting transfers between devices: 28.6 us -> 11.6 us  [the longest x4 10.6 us: chip_shift(): return lax.ppermute(part, 'ctx', moves)]
    ppermute x4 -> x8, waiting for transfers between devices: 14 us -> 27.3 us  [reduce_halves(): lax.ppermute(packed, 'ctx', [(2 * c + k, 2 * (c ^ 1 << bit) + k) for c in...]
    unnamed x74 -> x124, local copies, waits for them, and re-layouts: 11.9 us -> 25 us
    dynamic_update_slice x4 -> x0, other arithmetic: 12.2 us -> none  [on_device(): full_out = lax.dynamic_update_slice_in_dim(full_out, part, owner * shard, 1)]
    slice x0 -> x3, local copies, waits for them, and re-layouts: none -> 7.16 us  [the longest x1 6.04 us: on_device(): cut_weight[:, :, h].reshape(-1, count * sub)]
    ppermute x4 -> x8, starting transfers between devices: 15.9 us -> 12.3 us  [reduce_halves(): lax.ppermute(packed, 'ctx', [(2 * c + k, 2 * (c ^ 1 << bit) + k) for c in...]
    dot_general x20, matrix products: 38.4 us -> 35.4 us  [dot(): return jnp.einsum(spec, a, b, preferred_element_type=f32)]
  transfers between devices with their start and end apart: 23 -> 18, of which waited for: 7 -> 11; matrix products, arithmetic and copies ran while one was open for 36% -> 37% of each run, Pallas kernels for 0% -> 0%
where the time goes in v2:
time: 219 us; the launch traced here: 218 us
  matrix products  59 us (27%)
  waiting for transfers between devices  49.9 us (23%)
  local copies, waits for them, and re-layouts  41.8 us (19%)
  starting transfers between devices  24 us (11%)
  other arithmetic  22.3 us (10%)
  between operations  21.3 us (10%)
    dot_general x20, matrix products, dot(): return jnp.einsum(spec, a, b, preferred_element_type=f32)  35.4 us
    ppermute x8, waiting for transfers between devices, reduce_halves(): lax.ppermute(packed, 'ctx', [(2 * c + k, 2 * (c ^ 1 << bit) + k) for c in...  27.3 us
    unnamed x124, local copies, waits for them, and re-layouts  25 us
    ppermute x4, waiting for transfers between devices, chip_shift(): return lax.ppermute(part, 'ctx', moves)  18.1 us
    dot_general x2, matrix products, on_device(): lax.dot_general(whole, cut_weight[:, :, h].reshape(-1, count * sub), (((1...  13 us
    ppermute x8, starting transfers between devices, reduce_halves(): lax.ppermute(packed, 'ctx', [(2 * c + k, 2 * (c ^ 1 << bit) + k) for c in...  12.3 us
    dot_general x4, matrix products, product(): lax.dot_general(attended, jnp.concatenate(picked, axis=1), (((0,), (0,)),...  10.7 us
    ppermute x4, starting transfers between devices, chip_shift(): return lax.ppermute(part, 'ctx', moves)  10.6 us
  transfers between devices with their start and end apart: 18, of which 11 were waited for; matrix products, arithmetic and copies ran while one was open for 37% of the time, Pallas kernels for 0%

profile of v2, /device:TPU:0, one launch (start us, length us, event | category | flops | bytes accessed | tf_op | source)
XLA Modules:
  0.0 218.4 jit_solution(9687346483820487142)
XLA Ops:
  20.5 5.3 %fusion = (f32[8,512]{1,0:T(8,128)}, f32[8,512,512]{1,2,0:T(8,128)}) fusion(pred[512,512]{0,1:T(8,128)(4,1)S(1)} %fusion.72, bf16[8,2,512,16]{2,3,0,1:T(8,128)(2,1)S(1)} %bitcast.227), kind=kOutput, calls=%fused_computation.2 | convolution fusion | flops 81784832 | bytes 8929280 | tf_op jit(solution)/shard_map/hid,hjd->hij/dot_general | solution.py:48
  27.2 2.5 %copy.166 = bf16[64,8,8,128]{3,2,1,0:T(8,128)(2,1)} copy(bf16[64,8,8,128]{3,1,2,0:T(8,128)(2,1)} %bitcast.222) | data formatting | bytes 2097152
  33.1 4.4 %collective-permute-start.2 = (bf16[8,160,128]{2,0,1:T(8,128)(2,1)}, bf16[8,160,128]{2,0,1:T(8,128)(2,1)S(1)}, u32[]{:S(2)}, u32[]{:S(2)}) collective-permute-start(bf16[8,160,128]{2,0,1:T(8,128)(2,1)} %fusion.81), channel_id=1, source_target_pairs={{0,16},{4,20},{8,24},{12,28},{1,17},{5,21},{9,25},{13,29},{2,18},{... | collective-permute-start | bytes 983048 | tf_op jit(solution)/shard_map/ppermute | solution.py:76
  37.6 6.8 %fusion.70 = f32[8,512,128]{1,2,0:T(8,128)} fusion(bf16[8,512,128]{2,0,1:T(8,128)(2,1)S(1)} %bitcast.234, f32[8,512,512]{1,2,0:T(8,128)} %get-tuple-element.118, pred[512,512]{0,1:T(8,128)(4,1)S(1)} %copy-done.22), kind=kOutput, calls=%fused_computation.89 | convolution fusion | flops 551550976 | bytes 11796480 | tf_op jit(solution)/shard_map/hij,hjd->hid/dot_general | solution.py:48
  47.4 3.6 %collective-permute-start.1 = (bf16[8,160,128]{2,0,1:T(8,128)(2,1)}, bf16[8,160,128]{2,0,1:T(8,128)(2,1)S(1)}, u32[]{:S(2)}, u32[]{:S(2)}) collective-permute-start(bf16[8,160,128]{2,0,1:T(8,128)(2,1)} %fusion.81), channel_id=1, source_target_pairs={{0,8},{4,12},{8,16},{12,20},{16,24},{20,28},{1,9},{5,13},{9,17},{1... | collective-permute-start | bytes 983048 | tf_op jit(solution)/shard_map/ppermute | solution.py:76
  51.0 7.4 %collective-permute-done.1 = bf16[8,160,128]{2,0,1:T(8,128)(2,1)S(1)} collective-permute-done((bf16[8,160,128]{2,0,1:T(8,128)(2,1)}, bf16[8,160,128]{2,0,1:T(8,128)(2,1)S(1)}, u32[]{:S(2)}, u32[]{:S(2)}) %collective-permute-start.1) | collective-permute-done | bytes 327712 | tf_op jit(solution)/shard_map/ppermute | solution.py:76
  65.1 2.6 %constant_dynamic-slice_fusion.15 = (bf16[512,256]{0,1:T(8,128)(2,1)S(1)}, bf16[512,256]{0,1:T(8,128)(2,1)S(1)}, bf16[512,256]{0,1:T(8,128)(2,1)S(1)}, bf16[512,...) fusion(bf16[512,2048]{0,1:T(8,128)(2,1)} %all-gather.3.cloned.1, ...), kind=kLoop, calls=%fused_computation.253 | loop fusion | bytes 4194336 | tf_op jit(solution)/shard_map/dynamic_slice | solution.py:131
  67.7 2.7 %convolution_convert_fusion.1 = bf16[1024,1024]{1,0:T(8,128)(2,1)} fusion(bf16[512,1024]{0,1:T(8,128)(2,1)S(1)} %bitcast.218, bf16[512,256]{0,1:T(8,128)(2,1)S(1)} %get-tuple-element.61, bf16[512,256]{0,1:T(8,128)(2,1)S(1)} %get-tuple-element.62, bf16[512,256]{0,1:T(8,128)(2,1)S(1)} %get-tuple-element.63, bf16[512,256]{0,1:T(8,128)(2,1)S(1)} %get-tuple-element.64), kind=kOutput, calls=%fused_computation.33 | convolution fusion | flops 1078984704 | bytes 4194304 | tf_op jit(solution)/shard_map/dot_general | solution.py:136
  70.4 4.5 %collective-permute-done.3 = bf16[1024,1024]{1,0:T(8,128)(2,1)} collective-permute-done((bf16[1024,1024]{1,0:T(8,128)(2,1)}, bf16[1024,1024]{1,0:T(8,128)(2,1)}, u32[]{:S(2)}, u32[]{:S(2)}) %collective-permute-start.3) | collective-permute-done | bytes 2097184 | tf_op jit(solution)/shard_map/ppermute | solution.py:144
  74.9 5.4 %fusion.153 = (bf16[1024,1024]{1,0:T(8,128)(2,1)S(1)}, f32[1024,1024]{1,0:T(8,128)}) fusion(bf16[1024,1024]{1,0:T(8,128)(2,1)} %collective-permute-done.3, bf16[512,1024]{0,1:T(8,128)(2,1)} %bitcast.217, bf16[512,256]{0,1:T(8,128)(2,1)} %get-tuple-element.65, bf16[512,256]{0,1:T(8,128)(2,1)} %get-tuple-element.66, bf16[512,256]{0,1:T(8,128)(2,1)} %get-tuple-element.67, ...), kind=kOutput, calls=%fused_computation.295 | convolution fusion | flops 1081081856 | bytes 10485760 | tf_op jit(solution)/shard_map/dot_general | solution.py:136
  84.9 12.0 %copy.119 = bf16[1024,4096]{0,1:T(8,128)(2,1)} copy(bf16[1024,4096]{1,0:T(8,128)(2,1)} %param.23) | data formatting | bytes 16777216 | tf_op args[3]
  102.6 6.0 %fusion.146 = (bf16[1024,8,1,256]{0,3,2,1:T(8,128)(2,1)}, bf16[1024,8,1,256]{0,3,2,1:T(8,128)(2,1)}) fusion(bf16[1024,8,2,256]{0,3,2,1:T(8,128)(2,1)} %bitcast.215), kind=kLoop, calls=%fused_computation.288 | loop fusion | bytes 16777216 | tf_op jit(solution)/shard_map/slice | solution.py:239
  110.5 3.3 %collective-permute-done.6 = bf16[512,512]{1,0:T(8,128)(2,1)} collective-permute-done((bf16[512,512]{1,0:T(8,128)(2,1)}, bf16[512,512]{1,0:T(8,128)(2,1)}, u32[]{:S(2)}, u32[]{:S(2)}) %collective-permute-start.6) | collective-permute-done | bytes 524320 | tf_op jit(solution)/shard_map/ppermute | solution.py:157
  113.9 4.4 %collective-permute-done.5 = bf16[512,256]{1,0:T(8,128)(2,1)S(1)} collective-permute-done((bf16[512,256]{1,0:T(8,128)(2,1)}, bf16[512,256]{1,0:T(8,128)(2,1)S(1)}, u32[]{:S(2)}, u32[]{:S(2)}) %collective-permute-start.5) | collective-permute-done | bytes 262176 | tf_op jit(solution)/shard_map/ppermute | solution.py:157
  120.1 5.8 %fusion.155 = f32[512,1024]{1,0:T(8,128)} fusion(bf16[512,2048]{0,1:T(8,128)(2,1)S(1)} %copy-done.16, bf16[1024,2048]{0,1:T(8,128)(2,1)} %bitcast.224), kind=kOutput, calls=%fused_computation.297 | convolution fusion | flops 2147483648 | bytes 8388608 | tf_op jit(solution)/shard_map/dot_general | solution.py:237
  129.3 7.1 %convolution_add_fusion = f32[512,1024]{1,0:T(8,128)} fusion(f32[512,1024]{1,0:T(8,128)} %fusion.155, bf16[512,2048]{0,1:T(8,128)(2,1)} %all-gather.5.cloned.1.call-done, bf16[1024,2048]{0,1:T(8,128)(2,1)} %bitcast.216), kind=kOutput, calls=%fused_computation.34 | convolution fusion | flops 2148007936 | bytes 10485760 | tf_op jit(solution)/shard_map/dot_general | solution.py:237
  136.4 2.9 %copy.162 = f32[512,1024]{0,1:T(8,128)} copy(f32[512,1024]{1,0:T(8,128)} %convolution_add_fusion) | data formatting | bytes 4194304 | tf_op jit(solution)/shard_map/reshape | solution.py:246
  139.3 3.0 %divide_convert_fusion = (bf16[8,512,128]{1,2,0:T(8,128)(2,1)S(1)}, f32[8,512]{1,0:T(8,128)S(1)}) fusion(f32[8,512]{1,0:T(8,128)S(1)} %multiply_add_fusion.1, f32[8,512,128]{1,2,0:T(8,128)} %get-tuple-element.122, f32[512,1024]{0,1:T(8,128)} %copy.162), kind=kLoop, calls=%fused_computation.30 | loop fusion | flops 2617344 | bytes 5275648 | tf_op jit(solution)/shard_map/convert_element_type | solution.py:248
  142.4 4.7 %fusion.141 = f32[8,512,128]{1,2,0:T(8,128)S(1)} fusion(bf16[8,512,128]{1,2,0:T(8,128)(2,1)S(1)} %get-tuple-element.82, f32[8,512,512]{1,2,0:T(8,128)} %get-tuple-element.118, pred[512,512]{0,1:T(8,128)(4,1)S(1)} %copy-done.23), kind=kOutput, calls=%fused_computation.287 | convolution fusion | flops 551550976 | bytes 11796480 | tf_op jit(solution)/shard_map/hij,hid->hjd/dot_general | solution.py:48
  160.7 8.7 %collective-permute-done.10 = bf16[8,160,128]{2,0,1:T(8,128)(2,1)S(1)} collective-permute-done((bf16[8,160,128]{2,0,1:T(8,128)(2,1)S(1)}, bf16[8,160,128]{2,0,1:T(8,128)(2,1)S(1)}, u32[]{:S(2)}, u32[]{:S(2)}) %collective-permute-start.10) | collective-permute-done | bytes 327712 | tf_op jit(solution)/shard_map/ppermute | solution.py:76
  173.7 5.7 %collective-permute-start.12 = (bf16[512,512]{1,0:T(8,128)(2,1)S(1)}, bf16[512,512]{1,0:T(8,128)(2,1)S(1)}, u32[]{:S(2)}, u32[]{:S(2)}) collective-permute-start(bf16[512,512]{1,0:T(8,128)(2,1)S(1)} %pad_maximum_fusion.2), channel_id=1, source_target_pairs={{0,8},{4,12},{8,0},{12,4},{16,24},{20,28},{24,16},{28,20},{1,9},{5... | collective-permute-start | bytes 1572872 | tf_op jit(solution)/shard_map/ppermute | solution.py:157
  182.0 9.1 %collective-permute-done.12 = bf16[512,512]{1,0:T(8,128)(2,1)S(1)} collective-permute-done((bf16[512,512]{1,0:T(8,128)(2,1)S(1)}, bf16[512,512]{1,0:T(8,128)(2,1)S(1)}, u32[]{:S(2)}, u32[]{:S(2)}) %collective-permute-start.12) | collective-permute-done | bytes 524320 | tf_op jit(solution)/shard_map/ppermute | solution.py:157
  191.9 4.9 %collective-permute-done.14 = bf16[512,512]{1,0:T(8,128)(2,1)S(1)} collective-permute-done((bf16[512,512]{1,0:T(8,128)(2,1)S(1)}, bf16[512,512]{1,0:T(8,128)(2,1)S(1)}, u32[]{:S(2)}, u32[]{:S(2)}) %collective-permute-start.14) | collective-permute-done | bytes 524320 | tf_op jit(solution)/shard_map/ppermute | solution.py:157
  196.8 3.9 %collective-permute-done.13 = bf16[512,256]{1,0:T(8,128)(2,1)S(1)} collective-permute-done((bf16[512,256]{1,0:T(8,128)(2,1)S(1)}, bf16[512,256]{1,0:T(8,128)(2,1)S(1)}, u32[]{:S(2)}, u32[]{:S(2)}) %collective-permute-start.13) | collective-permute-done | bytes 262176 | tf_op jit(solution)/shard_map/ppermute | solution.py:157
  (241 shorter events, 70.3 us)
Async XLA Ops:
  7.2 57.9 %all-gather.3.cloned.1.call-start = ((), (), s32[]{:S(2)}) async-start(), calls=%async_computation | async-start | bytes 2621440 | tf_op jit(solution)/shard_map/all_gather | solution.py:187
  9.9 119.4 %all-gather.5.cloned.1.call-start = ((), (), s32[]{:S(2)}) async-start(), calls=%async_computation.1 | async-start | bytes 2621440 | tf_op jit(solution)/shard_map/all_gather | solution.py:187
  19.1 10.6 %collective-permute-start = (bf16[8,160,128]{2,0,1:T(8,128)(2,1)}, bf16[8,160,128]{2,0,1:T(8,128)(2,1)S(1)}, u32[]{:S(2)}, u32[]{:S(2)}) collective-permute-start(bf16[8,160,128]{2,0,1:T(8,128)(2,1)} %copy.128), channel_id=1, source_target_pairs={{0,4},{4,0},{8,12},{12,8},{16,20},{20,16},{24,28},{28,24},{1,5},{5... | collective-permute-start | bytes 983048 | tf_op jit(solution)/shard_map/ppermute | solution.py:99
  33.1 17.9 %collective-permute-start.2 = (bf16[8,160,128]{2,0,1:T(8,128)(2,1)}, bf16[8,160,128]{2,0,1:T(8,128)(2,1)S(1)}, u32[]{:S(2)}, u32[]{:S(2)}) collective-permute-start(bf16[8,160,128]{2,0,1:T(8,128)(2,1)} %fusion.81), channel_id=1, source_target_pairs={{0,16},{4,20},{8,24},{12,28},{1,17},{5,21},{9,25},{13,29},{2,18},{... | collective-permute-start | bytes 983048 | tf_op jit(solution)/shard_map/ppermute | solution.py:76
  46.8 11.8 %copy-start.42 = (f32[160]{0:T(256)S(1)}, f32[160]{0:T(256)}, u32[]{:S(2)}) copy-start(f32[160]{0:T(256)} %constant.125.clone) | copy-start | bytes 1924
  46.8 11.8 %copy-start.45 = (f32[160]{0:T(256)S(1)}, f32[160]{0:T(256)}, u32[]{:S(2)}) copy-start(f32[160]{0:T(256)} %constant.123.clone) | copy-start | bytes 1924
  46.8 11.8 %copy-start.51 = (f32[160]{0:T(256)S(1)}, f32[160]{0:T(256)}, u32[]{:S(2)}) copy-start(f32[160]{0:T(256)} %constant.126.clone) | copy-start | bytes 1924
  46.8 11.8 %copy-start.53 = (bf16[160]{0:T(256)(128)(2,1)S(1)}, bf16[160]{0:T(256)(128)(2,1)}, u32[]{:S(2)}) copy-start(bf16[160]{0:T(256)(128)(2,1)} %constant.127.clone) | copy-start | bytes 964
  47.4 13.7 %copy-start = (f32[160,8,512]{2,0,1:T(8,128)}, f32[160,8,512]{2,0,1:T(8,128)S(1)}, u32[]{:S(2)}) copy-start(f32[160,8,512]{2,0,1:T(8,128)S(1)} %fusion.106) | copy-start | bytes 7864324
  47.4 11.1 %collective-permute-start.1 = (bf16[8,160,128]{2,0,1:T(8,128)(2,1)}, bf16[8,160,128]{2,0,1:T(8,128)(2,1)S(1)}, u32[]{:S(2)}, u32[]{:S(2)}) collective-permute-start(bf16[8,160,128]{2,0,1:T(8,128)(2,1)} %fusion.81), channel_id=1, source_target_pairs={{0,8},{4,12},{8,16},{12,20},{16,24},{20,28},{1,9},{5,13},{9,17},{1... | collective-permute-start | bytes 983048 | tf_op jit(solution)/shard_map/ppermute | solution.py:76
  70.4 4.5 %collective-permute-start.3 = (bf16[1024,1024]{1,0:T(8,128)(2,1)}, bf16[1024,1024]{1,0:T(8,128)(2,1)}, u32[]{:S(2)}, u32[]{:S(2)}) collective-permute-start(bf16[1024,1024]{1,0:T(8,128)(2,1)} %convolution_convert_fusion.1), channel_id=1, source_target_pairs={{0,4},{4,0},{8,12},{12,8},{16,20},{20,16},{24,28},{28,24},{1,5},{5... | collective-permute-start | bytes 6291464 | tf_op jit(solution)/shard_map/ppermute | solution.py:144
  82.5 16.2 %collective-permute-start.4 = (bf16[512,512]{1,0:T(8,128)(2,1)}, bf16[512,512]{1,0:T(8,128)(2,1)}, u32[]{:S(2)}, u32[]{:S(2)}) collective-permute-start(bf16[512,512]{1,0:T(8,128)(2,1)} %pad_maximum_fusion.1), channel_id=1, source_target_pairs={{0,8},{4,12},{8,0},{12,4},{16,24},{20,28},{24,16},{28,20},{1,9},{5... | collective-permute-start | bytes 1572872 | tf_op jit(solution)/shard_map/ppermute | solution.py:157
  98.7 15.1 %collective-permute-start.6 = (bf16[512,512]{1,0:T(8,128)(2,1)}, bf16[512,512]{1,0:T(8,128)(2,1)}, u32[]{:S(2)}, u32[]{:S(2)}) collective-permute-start(bf16[512,512]{1,0:T(8,128)(2,1)} %slice.398), channel_id=1, source_target_pairs={{0,16},{4,20},{8,24},{12,28},{16,0},{20,4},{24,8},{28,12},{1,17},{... | collective-permute-start | bytes 1572872 | tf_op jit(solution)/shard_map/ppermute | solution.py:157
  100.6 17.6 %collective-permute-start.5 = (bf16[512,256]{1,0:T(8,128)(2,1)}, bf16[512,256]{1,0:T(8,128)(2,1)S(1)}, u32[]{:S(2)}, u32[]{:S(2)}) collective-permute-start(bf16[512,256]{1,0:T(8,128)(2,1)} %fusion.95), channel_id=1, source_target_pairs={{0,16},{4,20},{8,24},{12,28},{16,0},{20,4},{24,8},{28,12},{1,17},{... | collective-permute-start | bytes 786440 | tf_op jit(solution)/shard_map/ppermute | solution.py:157
  119.7 7.4 %collective-permute-start.7 = (bf16[512,256]{1,0:T(8,128)(2,1)S(1)}, bf16[512,256]{1,0:T(8,128)(2,1)S(1)}, u32[]{:S(2)}, u32[]{:S(2)}) collective-permute-start(bf16[512,256]{1,0:T(8,128)(2,1)S(1)} %get-tuple-element.47), channel_id=1, source_target_pairs={{0,8},{4,12},{8,0},{12,4},{16,24},{20,28},{24,16},{28,20},{1,9},{5... | collective-permute-start | bytes 786440 | tf_op jit(solution)/shard_map/ppermute | solution.py:157
  152.6 4.2 %collective-permute-start.8 = (bf16[8,160,128]{2,0,1:T(8,128)(2,1)S(1)}, bf16[8,160,128]{2,0,1:T(8,128)(2,1)S(1)}, u32[]{:S(2)}, u32[]{:S(2)}) collective-permute-start(bf16[8,160,128]{2,0,1:T(8,128)(2,1)S(1)} %fusion.79), channel_id=1, source_target_pairs={{0,4},{4,0},{8,12},{12,8},{16,20},{20,16},{24,28},{28,24},{1,5},{5... | collective-permute-start | bytes 983048 | tf_op jit(solution)/shard_map/ppermute | solution.py:99
  154.2 18.1 %collective-permute-start.11 = (bf16[1024,1024]{1,0:T(8,128)(2,1)S(1)}, bf16[1024,1024]{1,0:T(8,128)(2,1)S(1)}, u32[]{:S(2)}, u32[]{:S(2)}) collective-permute-start(bf16[1024,1024]{1,0:T(8,128)(2,1)S(1)} %convolution_convert_fusion), channel_id=1, source_target_pairs={{0,4},{4,0},{8,12},{12,8},{16,20},{20,16},{24,28},{28,24},{1,5},{5... | collective-permute-start | bytes 6291464 | tf_op jit(solution)/shard_map/ppermute | solution.py:144
  157.4 11.9 %collective-permute-start.10 = (bf16[8,160,128]{2,0,1:T(8,128)(2,1)S(1)}, bf16[8,160,128]{2,0,1:T(8,128)(2,1)S(1)}, u32[]{:S(2)}, u32[]{:S(2)}) collective-permute-start(bf16[8,160,128]{2,0,1:T(8,128)(2,1)S(1)} %fusion.77), channel_id=1, source_target_pairs={{16,0},{20,4},{24,8},{28,12},{17,1},{21,5},{25,9},{29,13},{18,2},{... | collective-permute-start | bytes 983048 | tf_op jit(solution)/shard_map/ppermute | solution.py:76
  159.4 11.9 %collective-permute-start.9 = (bf16[8,160,128]{2,0,1:T(8,128)(2,1)S(1)}, bf16[8,160,128]{2,0,1:T(8,128)(2,1)S(1)}, u32[]{:S(2)}, u32[]{:S(2)}) collective-permute-start(bf16[8,160,128]{2,0,1:T(8,128)(2,1)S(1)} %fusion.77), channel_id=1, source_target_pairs={{8,0},{12,4},{16,8},{20,12},{24,16},{28,20},{9,1},{13,5},{17,9},{2... | collective-permute-start | bytes 983048 | tf_op jit(solution)/shard_map/ppermute | solution.py:76
  173.6 27.1 %copy-start.2 = (f32[1024,1024]{1,0:T(8,128)}, f32[1024,1024]{1,0:T(8,128)S(1)}, u32[]{:S(2)}) copy-start(f32[1024,1024]{1,0:T(8,128)S(1)} %get-tuple-element.126) | copy-start | bytes 12582916
  173.7 17.4 %collective-permute-start.12 = (bf16[512,512]{1,0:T(8,128)(2,1)S(1)}, bf16[512,512]{1,0:T(8,128)(2,1)S(1)}, u32[]{:S(2)}, u32[]{:S(2)}) collective-permute-start(bf16[512,512]{1,0:T(8,128)(2,1)S(1)} %pad_maximum_fusion.2), channel_id=1, source_target_pairs={{0,8},{4,12},{8,0},{12,4},{16,24},{20,28},{24,16},{28,20},{1,9},{5... | collective-permute-start | bytes 1572872 | tf_op jit(solution)/shard_map/ppermute | solution.py:157
  181.9 14.9 %collective-permute-start.14 = (bf16[512,512]{1,0:T(8,128)(2,1)S(1)}, bf16[512,512]{1,0:T(8,128)(2,1)S(1)}, u32[]{:S(2)}, u32[]{:S(2)}) collective-permute-start(bf16[512,512]{1,0:T(8,128)(2,1)S(1)} %slice.438), channel_id=1, source_target_pairs={{0,16},{4,20},{8,24},{12,28},{16,0},{20,4},{24,8},{28,12},{1,17},{... | collective-permute-start | bytes 1572872 | tf_op jit(solution)/shard_map/ppermute | solution.py:157
  191.1 9.6 %collective-permute-start.13 = (bf16[512,256]{1,0:T(8,128)(2,1)S(1)}, bf16[512,256]{1,0:T(8,128)(2,1)S(1)}, u32[]{:S(2)}, u32[]{:S(2)}) collective-permute-start(bf16[512,256]{1,0:T(8,128)(2,1)S(1)} %fusion.91), channel_id=1, source_target_pairs={{0,16},{4,20},{8,24},{12,28},{16,0},{20,4},{24,8},{28,12},{1,17},{... | collective-permute-start | bytes 786440 | tf_op jit(solution)/shard_map/ppermute | solution.py:157
  201.6 7.1 %collective-permute-start.15 = (bf16[512,256]{1,0:T(8,128)(2,1)}, bf16[512,256]{1,0:T(8,128)(2,1)}, u32[]{:S(2)}, u32[]{:S(2)}) collective-permute-start(bf16[512,256]{1,0:T(8,128)(2,1)} %get-tuple-element.45), channel_id=1, source_target_pairs={{0,8},{4,12},{8,0},{12,4},{16,24},{20,28},{24,16},{28,20},{1,9},{5... | collective-permute-start | bytes 786440 | tf_op jit(solution)/shard_map/ppermute | solution.py:157
  (53 other events, 210.3 us)
Sparse Core Ops, SparseCore 0:
  10.0 48.3 all-gather.2
  70.5 46.9 all-gather.4
